TPU v7x, 32 devices: a whole 2x2x4 slice. The times are simulated.
32 devices in a mesh: die: 4 (over y, x), tile: 8 (over z, core).
Axes of the slice: x: 2, y: 2, z: 4, core: 2. Of those that a mesh axis runs over, the one named last changes fastest.
Arguments:
- source_heating: float32 [16, 128, 2048], P('die', 'tile'), may hold values from -96 to 96, as said below
- material_thermal_values: float32 [6], replicated, may hold values from 0.5 to 8
- layer_material: int32 [16], P('die'), may hold values from 0 to 5
- via_conductance: float32 [4], P('die'), may hold values from 2 to 16
- via_blocks: int32 [4, 24, 4], P('die'), may hold values from 0 to 2048, as said below
Outputs:
- thermal_solution: float32 [16, 128, 2048], P('die', 'tile')
- balance_defect: float32 [16, 128, 2048], P('die', 'tile')
Inputs may be any that keep to these rules, and one draw needn't show every extreme that they name: `via_blocks`: entry (d, b) is (first row, first column, height, width) of via block b on top of die d, joining die d's top layer to die d + 1's bottom layer, or to the cooled lid for the top die. Height is 8, 16 or 32 and width 16, 32 or 64, each cut to the plane's 128 x 2048 cells; every block lies inside the plane; blocks may intersect. `source_heating`: heat per cell.
All inputs are finite; a program needn't handle non-finite values.
Results may differ from a plain program's by a relative error of at most 0.0003.
Values sent between devices are 32-bit elements; how exact they have to be, the bound alone decides.
No kernel may reach another device: no remote copies, remote signals or barrier semaphores. Data moves between devices by JAX's collectives and lax.ppermute only.
A program may use at most 128 MiB of HBM per device.

v0:
```python
import functools

import jax
import jax.numpy as jnp
import numpy as np
from jax import lax
from jax.experimental import pallas as pl
from jax.experimental.pallas import tpu as pltpu
from jax.sharding import PartitionSpec as P


OMEGA = 0.8
NC = 6
LN = 128
HX = 64
VMEM = 67_043_328
HY = 8
F32 = jnp.float32
BF16 = jnp.bfloat16


def iota(shape, axis):
    return lax.broadcasted_iota(jnp.int32, shape, axis)


def split_dot(x, m):
    hi = x.astype(BF16)
    lo = (x - hi.astype(F32)).astype(BF16)
    return jnp.dot(hi, m, preferred_element_type=F32) + jnp.dot(lo, m, preferred_element_type=F32)


def pair_dot(a, b):
    return lax.dot_general(a, b, (((0,), (0,)), ((), ())), preferred_element_type=F32)


class Sizes:
    def __init__(self, mesh_shape, f_shape, n_blocks):
        self.nd, self.nt = mesh_shape["die"], mesh_shape["tile"]
        self.lz, self.rows, self.width = f_shape
        self.nb = n_blocks
        self.wc = self.width // self.nd
        self.we = self.wc + LN
        self.j0 = self.we // LN
        self.nz = self.nd * self.lz
        self.re = self.rows + 2 * HY
        self.own1 = self.rows // 4
        self.r1 = self.re // 4
        self.c1 = self.wc // 4
        self.e1 = 2 * self.r1
        self.pad1 = (self.e1 - self.own1) // 2
        self.j1 = 2
        self.w1 = self.j1 * LN
        self.c2 = self.wc // 16
        self.part = self.lz * self.j0 * self.rows
        assert self.rows == 16 and self.lz == 4 and self.c1 == LN
        assert self.nd * self.c2 == LN and self.nb <= LN and self.nt <= LN and self.nt % 8 == 0


def place():
    return lax.axis_index("die"), lax.axis_index("tile")


def even():
    _, t = place()
    return lax.rem(t, 2) == 0


def tiles(j):
    return slice(j * LN, (j + 1) * LN)


def windows(lo, hi):
    return [min(r, hi - 8) for r in range(lo, hi, 8)]


def pack_kernel(s, mat_h, material_h, conductance_h, blocks_h, f_h, *refs):
    outs, (mat, material, conductance, blocks, f, sem) = refs[: s.nd], refs[s.nd :]
    pairs = [(f_h, f), (mat_h, mat), (material_h, material), (conductance_h, conductance), (blocks_h, blocks)]
    copies = [pltpu.make_async_copy(a, b, sem.at[k]) for k, (a, b) in enumerate(pairs)]
    for c in copies:
        c.start()
    for c in copies[1:]:
        c.wait()
    d, _ = place()
    lane, sub = iota((8, LN), 1), iota((8, LN), 0)
    info = jnp.where((sub == 5) & (lane == 0), conductance[0, 0], 0.0)
    for z in range(s.lz):
        info = jnp.where((sub == 4) & (lane == z), mat[material[z]], info)
    for out in outs:
        out[s.part :, :] = info
        out[s.part : s.part + 4, : s.nb] = blocks[...].astype(F32)
    copies[0].wait()
    low = iota((s.rows, LN), 1) < HX
    for step, out in enumerate(outs):
        e = lax.rem(d + step, s.nd)
        right = lax.rem(e + 1, s.nd) * s.wc
        left = lax.rem(e + s.nd - 1, s.nd) * s.wc + (s.wc - LN)

        def column(z, at):
            return f[z, :, pl.ds(pl.multiple_of(at, LN), LN)]

        for z in range(s.lz):
            for j in range(s.j0):
                at = (z * s.j0 + j) * s.rows
                if j < s.j0 - 1:
                    x = column(z, e * s.wc + j * LN)
                else:
                    x = jnp.where(low, column(z, right), column(z, left))
                out[at : at + s.rows, :] = x


def assemble_kernel(s, *refs):
    parts, (one, two, prm) = refs[: s.nd], refs[s.nd :]
    d, _ = place()
    n = s.lz * s.j0
    lower = even()
    for step, part in enumerate(parts):
        e = lax.rem(d + s.nd - step, s.nd)
        for q in range(n):
            top = part[q * s.rows : q * s.rows + HY, :]
            bot = part[q * s.rows + HY : (q + 1) * s.rows, :]
            one[n * e + q] = jnp.where(lower, bot, top)
            two[n * e + q] = jnp.where(lower, top, bot)
        prm[e] = part[s.part :, :]


def overlap(lo, size, first, past):
    return jnp.maximum(jnp.minimum(lo + size, past) - jnp.maximum(lo, first), 0.0)


def block_bounds(s, info):
    b = jnp.transpose(info)
    lane = iota((LN, 8), 1)
    col = [jnp.sum(jnp.where(lane == k, b, 0.0), axis=1, keepdims=True) for k in range(4)]
    col = [x[: s.nb] for x in col]
    return col[0], col[0] + col[2], col[1], col[1] + col[3]


def die_values(s, prm):
    lane8, sub8 = iota((8, LN), 1), iota((8, LN), 0)

    def pick(tile, row, col):
        return jnp.sum(jnp.where((lane8 == col) & (sub8 == row), tile, 0.0), keepdims=True)

    info = [prm[g] for g in range(s.nd)]
    cond = [pick(info[z // s.lz], 4, z % s.lz) for z in range(s.nz)]
    via = [pick(info[g], 5, 0) for g in range(s.nd)]
    vert = [2.0 * p * q / (p + q) for p, q in zip(cond, cond[1:] + cond[-1:])]
    return cond, vert, via, [block_bounds(s, x) for x in info]


def level_coeffs(s, level, values, via_up, via_down, scale):
    cond, vert, via, blocks = values
    d, t = place()
    size = 4**level
    n, own = (s.we, s.wc) if level == 0 else (s.w1, s.c1)
    height, nj = (s.re, s.j0) if level == 0 else (s.e1, s.j1)
    pad = HY if level == 0 else s.pad1
    halo = HX // size

    def columns(shape, axis):
        p = iota(shape, axis)
        return p, d * own + jnp.where(p >= n - halo, p - n, p)

    first = t * (s.rows // size) - pad
    row = ((first + iota((1, LN), 1)) * size).astype(F32)
    col = (columns((1, n), 1)[1] * size).astype(F32)
    rr = first + iota((height, n), 0)
    pp, cc = columns((height, n), 1)
    inside = (rr >= 0) & (rr < s.rows * s.nt // size) & (cc >= 0) & (cc < s.width // size)
    inside = jnp.where(inside & ((pp < own + halo) | (pp >= n - halo)), OMEGA, 0.0)
    via_down[0] = jnp.zeros(via_down.shape[1:], F32)
    for g in range(s.nd):
        r0, r1, c0, c1 = blocks[g]
        m = pair_dot(
            overlap(row, float(size), r0, r1).astype(BF16), overlap(col, float(size), c0, c1).astype(BF16)
        )[:height]
        top = (g + 1) * s.lz - 1
        m = m * (via[g] * (0.25**level))
        for j in range(nj):
            via_up[g, j] = m[:, tiles(j)] / cond[top]
            if g + 1 < s.nd:
                via_down[g + 1, j] = m[:, tiles(j)] / cond[top + 1]
    for z in range(s.nz):
        g, a = z // s.lz, z % s.lz
        const = 4.0
        if a < s.lz - 1:
            const = const + vert[z] * (4.0**level) / cond[z]
        if a > 0:
            const = const + vert[z - 1] * (4.0**level) / cond[z]
        for j in range(nj):
            diag = const
            if a == s.lz - 1:
                diag = diag + via_up[g, j]
            if a == 0:
                diag = diag + via_down[g, j]
            scale[z, j] = inside[:, tiles(j)] / diag


def coeff_fine_kernel(s, prm, up0, down0, e0, c, ic, cu, cd):
    values = die_values(s, prm)
    cond, vert = values[:2]
    for z in range(s.nz):
        c[z] = jnp.zeros((8, LN), F32) + cond[z]
        ic[z] = jnp.zeros((8, LN), F32) + 1.0 / cond[z]
        cu[z] = jnp.zeros((8, LN), F32) + vert[z] / cond[z]
        cd[z] = jnp.zeros((8, LN), F32) + vert[max(z - 1, 0)] / cond[z]
    level_coeffs(s, 0, values, up0, down0, e0)


def coeff_coarse_kernel(s, prm, up1, down1, e1, u2, l2, e2):
    values = die_values(s, prm)
    cond, vert, via, blocks = values
    level_coeffs(s, 1, values, up1, down1, e1)
    group = iota((1, LN), 1) // s.c2
    xin = iota((1, LN), 1) % s.c2

    def by_group(values):
        out = jnp.zeros((1, LN), F32)
        for g in range(s.nd):
            out = jnp.where(group == g, values[g], out)
        return out

    cl = [by_group([cond[s.lz * g + a] for g in range(s.nd)]) * 16.0 for a in range(s.lz)]
    vl = [by_group([vert[s.lz * g + a] for g in range(s.nd)]) * 256.0 for a in range(s.lz)]
    vial = by_group(via)
    row2 = (iota((1, LN), 1) * 16).astype(F32)
    ra = jnp.concatenate([overlap(row2, 16.0, b[0], b[1]) for b in blocks], axis=0).astype(BF16)
    zero2 = jnp.zeros((s.nt, LN), F32)
    for e in range(s.nd):
        col2 = ((e * s.c2 + xin) * 16).astype(F32)
        cb = jnp.concatenate(
            [jnp.where(group == g, overlap(col2, 16.0, b[2], b[3]), 0.0) for g, b in enumerate(blocks)],
            axis=0,
        ).astype(BF16)
        v2 = pair_dot(ra, cb)[: s.nt] * vial
        ups = [zero2 + vl[a] for a in range(s.lz - 1)] + [v2]
        first = jnp.where(iota((s.nt, LN), 1) >= s.c2, pltpu.roll(v2, s.c2, 1), 0.0)
        lows = [first] + ups[:-1]
        for a in range(s.lz):
            q = e * s.lz + a
            u2[q] = ups[a] / cl[a]
            l2[q] = lows[a] / cl[a]
            e2[q] = OMEGA * cl[a] / (4.0 * cl[a] + ups[a] + lows[a])


class Level:
    def __init__(self, s, level, up, down, scale, cu, cd):
        self.s, self.up, self.down, self.scale, self.cu, self.cd = s, up, down, scale, cu, cd
        self.nj = (s.j0, s.j1)[level]
        self.us = 4.0**level

    def walk(self, src, f, lo, hi, emit, count=None):
        s, n = self.s, self.nj
        lane = iota((8, LN), 1)
        first, last = lane == 0, lane == LN - 1

        def group(g, carry):
            for a in range(s.lz):
                z = g * s.lz + a
                for r in windows(lo, hi):
                    rows = pl.ds(r, 8)
                    v = [src[z + 1, j, rows, :] for j in range(n)]
                    ahead = [pltpu.roll(x, LN - 1, 1) for x in v]
                    behind = [pltpu.roll(x, 1, 1) for x in v]
                    for j in range(count or n):
                        k_up = self.cu[z] * self.us if a < s.lz - 1 else self.up[g, j, rows, :]
                        k_down = self.cd[z] * self.us if a > 0 else self.down[g, j, rows, :]
                        x = jnp.where(last, ahead[(j + 1) % n], ahead[j]) + jnp.where(first, behind[j - 1], behind[j])
                        y = src[z + 1, j, pl.ds(r - 1, 8), :] + src[z + 1, j, pl.ds(r + 1, 8), :]
                        x = (f[z, j, rows, :] + x) + y
                        x = x + (k_up * src[z + 2, j, rows, :] + k_down * src[z, j, rows, :])
                        emit(z, j, rows, v[j], x, k_up, k_down)
            return carry

        lax.fori_loop(0, s.nd, group, 0)

    def sweep(self, src, dst, f, lo, hi):
        def emit(z, j, rows, v, g, *_):
            dst[z + 1, j, rows, :] = (1.0 - OMEGA) * v + self.scale[z, j, rows, :] * g

        self.walk(src, f, lo, hi, emit)

    def residual(self, src, f, lo, hi, put, count=None):
        def emit(z, j, rows, v, g, k_up, k_down):
            put(z, j, rows, g - (4.0 + k_up + k_down) * v)

        self.walk(src, f, lo, hi, emit, count)


def zero_ends(s, *bufs):
    for b in bufs:
        b[0] = jnp.zeros(b.shape[1:], F32)
        b[s.nz + 1] = jnp.zeros(b.shape[1:], F32)


def restrict(s, level, src, f, lo, hi, down, rbuf, sums, r1):
    for k in range(s.nz * s.j0):
        rbuf[k * s.re : k * s.re + 8, :] = jnp.zeros((8, LN), F32)
        rbuf[(k + 1) * s.re - 8 : (k + 1) * s.re, :] = jnp.zeros((8, LN), F32)

    def put(z, j, rows, x):
        rbuf[pl.ds((z * s.j0 + j) * s.re + rows.start, 8), :] = x

    level.residual(src, f, lo, hi, put)

    def body(z, carry):
        for j in range(s.j0):
            part = [rbuf[pl.ds((z * s.j0 + j) * s.re + k, s.r1, stride=4), :] for k in range(4)]
            sums[z, :, tiles(j)] = (part[0] + part[1]) + (part[2] + part[3])
        return carry

    lax.fori_loop(0, s.nz, body, 0)
    out = split_dot(sums[...].reshape(s.nz * s.r1, s.we), down[...])
    for z in range(s.nz):
        for j in range(s.j1):
            r1[z, j] = out[z * s.r1 : (z + 1) * s.r1, tiles(j)]


def down_kernel(s, out):
    p, q = iota((s.we, s.w1), 0), iota((s.we, s.w1), 1)
    at = p // 4 + jnp.where(p >= s.wc + HX, s.w1 - s.we // 4, 0)
    out[...] = jnp.where(at == q, 0.25, 0.0).astype(BF16)


def fine_first_kernel(s, from_one, from_two, one, two, up0, down0, e0, ic, cu, cd, down, f, v2, r1, va, rbuf, sums):
    level = Level(s, 0, up0, down0, e0, cu, cd)
    lower = even()
    zero_ends(s, va, v2)

    def body(z, carry):
        for k, (a, b) in enumerate(((from_two, from_one), (two, one), (one, two), (from_one, from_two))):
            rows = slice(k * HY, (k + 1) * HY)
            for j in range(s.j0):
                q = z * s.j0 + j
                x = jnp.where(lower, a[q], b[q]) * ic[z]
                f[z, j, rows, :] = x
                va[z + 1, j, rows, :] = e0[z, j, rows, :] * x
        return carry

    lax.fori_loop(0, s.nz, body, 0)
    level.sweep(va, v2, f, 1, s.re - 1)
    restrict(s, level, v2, f, HY - 4, s.re - HY + 4, down, rbuf, sums, r1)


def middle_first_kernel(s, r1a, r1, r1b, up1, down1, e1, cu, cd, down2, rx, w2, send, wa, buf):
    level = Level(s, 1, up1, down1, e1, cu, cd)
    half, own, pad = s.r1, s.own1, s.pad1
    sub = iota((half, LN), 0)
    lower = even()
    zero_ends(s, wa, w2)

    def body(z, carry):
        for j in range(s.j1):
            mid = pltpu.roll(r1[z, j], half // 2, 0)
            up = jnp.where(sub >= pad, mid, jnp.where(lower, r1b[z, j], r1a[z, j]))
            down = jnp.where(sub < own - (half - pad), mid, jnp.where(lower, r1a[z, j], r1b[z, j]))
            rx[z, j, :half, :] = up
            rx[z, j, half:, :] = down
            wa[z + 1, j, :half, :] = e1[z, j, :half, :] * up
            wa[z + 1, j, half:, :] = e1[z, j, half:, :] * down
        return carry

    lax.fori_loop(0, s.nz, body, 0)
    level.sweep(wa, w2, rx, pad - 4, pad + own + 4)

    def put(z, j, rows, x):
        buf[pl.ds(pl.multiple_of(z * 8, 8), 8), :] = x

    level.residual(w2, rx, pad - 2, pad + own + 2, put, 1)
    sub8, group = iota((8, LN), 0), iota((8, LN), 1) // s.c2
    tile = jnp.zeros((8, LN), F32)
    for h in range(s.nz // 8):
        part = [buf[pl.ds(64 * h + 2 + k, 8, stride=8), :] for k in range(own)]
        x = split_dot((part[0] + part[1]) + (part[2] + part[3]), down2[...])
        y = pltpu.roll(x, 4, 0)
        for g in (2 * h, 2 * h + 1):
            tile = jnp.where(group == g, jnp.where((sub8 < 4) == (g % 2 == 0), x, y), tile)
    for k in range(s.nd * s.nt * s.lz // 8):
        send[8 * k : 8 * k + 8, :] = tile


def coarse(s, got, u2, l2, e2, cs):
    lane = iota((s.nt, LN), 1)
    x, t = lane % s.c2, iota((s.nt, LN), 0)
    first_x, last_x = x == 0, x == s.c2 - 1
    slabs = s.nd * s.lz
    rhs, v = [], []
    for q in range(slabs):
        e, a = q // s.lz, q % s.lz
        r = got[pl.ds(e * s.nt * s.lz + a, s.nt, stride=s.lz), :]
        rhs.append(r)
        v.append(e2[q] * r)
    zero = jnp.zeros((s.nt, LN), F32)

    def body(_, v):
        new = []
        for q in range(slabs):
            e, a = q // s.lz, q % s.lz
            w = v[q]
            right = pltpu.roll(v[q + s.lz], s.c2 - 1, 1) if e < s.nd - 1 else zero
            left = pltpu.roll(v[q - s.lz], LN - (s.c2 - 1), 1) if e > 0 else zero
            side = jnp.where(last_x, right, pltpu.roll(w, LN - 1, 1))
            side += jnp.where(first_x, left, pltpu.roll(w, 1, 1))
            side += jnp.where(t == s.nt - 1, 0.0, pltpu.roll(w, s.nt - 1, 0))
            side += jnp.where(t == 0, 0.0, pltpu.roll(w, 1, 0))
            if a < s.lz - 1:
                up = v[q + 1]
            else:
                up = jnp.where(lane >= LN - s.c2, 0.0, pltpu.roll(v[q - a], LN - s.c2, 1))
            if a > 0:
                down = v[q - 1]
            else:
                down = jnp.where(lane < s.c2, 0.0, pltpu.roll(v[q + s.lz - 1], s.c2, 1))
            g = (rhs[q] + side) + (u2[q] * up + l2[q] * down)
            new.append((1.0 - OMEGA) * w + e2[q] * g)
        return tuple(new)

    v = lax.fori_loop(0, NC - 1, body, tuple(v))
    for q in range(slabs):
        cs[q, :HY, :] = jnp.zeros((HY, LN), F32)
        cs[q, HY + s.nt :, :] = jnp.zeros((HY, LN), F32)
        cs[q, HY : HY + s.nt, :] = v[q]


def middle_last(s, level, cs, spread2, w2, rx, comp, wide, wa, wb):
    d, t = place()
    lane, upper = iota((8, LN), 1), iota((8, LN), 0) < 4
    after = lax.rem(d + 1, s.nd) * s.lz
    before = lax.rem(d + s.nd - 1, s.nd) * s.lz
    zero_ends(s, wa, wb)
    for a in range(s.lz):
        rows = [cs[base + a, pl.ds(HY - 1 + t, 8), :] for base in (d * s.lz, after, before)]
        for g in range(s.nd):
            turn = []
            for r, by in zip(rows, (0, s.c2, LN - s.c2)):
                by = (by - g * s.c2) % LN
                turn.append(pltpu.roll(r, by, 1) if by else r)
            z = g * s.lz + a
            comp[8 * z : 8 * z + 8, :] = jnp.where(
                lane < s.c2, turn[0], jnp.where(lane < LN // 2, turn[1], turn[2])
            )
    wide[...] = split_dot(comp[...], spread2[...]).reshape(wide.shape)

    def body(z, carry):
        x = [[wide[z, k : k + 1, tiles(j)] for k in range(3)] for j in range(s.j1)]
        for k in range(2):
            rows = slice(s.pad1 - 4 + 4 * k, s.pad1 + 4 + 4 * k)
            for j in range(s.j1):
                y = w2[z + 1, j, rows, :] + jnp.where(upper, x[j][k], x[j][k + 1])
                wa[z + 1, j, rows, :] = jnp.where(level.scale[z, j, rows, :] > 0.0, y, 0.0)
        return carry

    lax.fori_loop(0, s.nz, body, 0)
    level.sweep(wa, wb, rx, s.pad1 - 3, s.pad1 + s.own1 + 3)
    level.sweep(wb, wa, rx, s.pad1 - 2, s.pad1 + s.own1 + 2)


def correct_fine(s, w, v, spread1, wide, dst):
    rows = slice(s.pad1 - 2, s.pad1 + s.own1 + 2)
    lhs = jnp.concatenate([w[1 : s.nz + 1, j, rows, :].reshape(s.nz * s.r1, LN) for j in range(s.j1)], axis=1)
    wide[...] = split_dot(lhs, spread1[...]).reshape(wide.shape)
    upper = iota((8, LN), 0) < 4

    def body(z, carry):
        for k in range(s.r1 // 2):
            rows = slice(8 * k, 8 * k + 8)
            for j in range(s.j0):
                x = [wide[z, 2 * k + i : 2 * k + i + 1, tiles(j)] for i in range(2)]
                dst[z + 1, j, rows, :] = v[z + 1, j, rows, :] + jnp.where(upper, x[0], x[1])
        return carry

    lax.fori_loop(0, s.nz, body, 0)


def back_kernel(
    s, got, v2, f, w2, rx,
    u2, l2, e2, up1, down1, e1, up0, down0, e0, cu, cd, spread2, spread1, down,
    v, r1, cs, comp, wide2, wa, wb, va, vb, wide, rbuf,
):
    fine = Level(s, 0, up0, down0, e0, cu, cd)
    middle = Level(s, 1, up1, down1, e1, cu, cd)
    zero_ends(s, va, vb, v)
    coarse(s, got, u2, l2, e2, cs)
    middle_last(s, middle, cs, spread2, w2, rx, comp, wide2, wa, wb)
    correct_fine(s, wa, v2, spread1, wide, va)
    fine.sweep(va, vb, f, 2, s.re - 2)
    fine.sweep(vb, va, f, 3, s.re - 3)
    fine.sweep(va, vb, f, 4, s.re - 4)
    fine.sweep(vb, v, f, 5, s.re - 5)
    restrict(s, fine, v, f, HY, HY + s.rows, down, rbuf, wide, r1)


def last_kernel(
    s, got, w2, rx, v2, f, u2, l2, e2, up1, down1, e1, up0, down0, e0, cu, cd, spread2, spread1, *refs,
):
    outs, (cs, comp, wide2, wa, wb, va, vb, wide) = refs[: s.nd], refs[s.nd :]
    fine = Level(s, 0, up0, down0, e0, cu, cd)
    middle = Level(s, 1, up1, down1, e1, cu, cd)
    d, _ = place()
    zero_ends(s, va, vb)
    coarse(s, got, u2, l2, e2, cs)
    middle_last(s, middle, cs, spread2, w2, rx, comp, wide2, wa, wb)
    correct_fine(s, wa, v2, spread1, wide, va)
    fine.sweep(va, vb, f, HY - 2, HY + s.rows + 2)
    fine.sweep(vb, va, f, HY - 1, HY + s.rows + 1)

    nj = s.j0 - 1
    for step, out in enumerate(outs):
        e = lax.rem(d + step, s.nd)
        for k in range(s.lz + 2):
            for j in range(nj):
                at = (k * nj + j) * s.rows
                out[at : at + s.rows, :] = va[s.lz * e + k, j, HY : HY + s.rows, :]
        for a in range(s.lz):
            for j in range(nj):
                at = (s.lz + 2) * nj * s.rows + (a * nj + j) * 2
                out[at : at + 1, :] = va[s.lz * e + a + 1, j, HY - 1 : HY, :]
                out[at + 1 : at + 2, :] = va[s.lz * e + a + 1, j, HY + s.rows : HY + s.rows + 1, :]


def coeff_own_kernel(s, prm, up, down):
    d, t = place()
    lane8, sub8 = iota((8, LN), 1), iota((8, LN), 0)
    row = (t * s.rows + iota((1, LN), 1)).astype(F32)
    col = iota((1, s.width), 1).astype(F32)
    for k, out in enumerate((up, down)):
        info = prm[lax.rem(d + s.nd - k, s.nd)]
        via = jnp.sum(jnp.where((lane8 == 0) & (sub8 == 5), info, 0.0), keepdims=True)
        if k == 1:
            via = via * (d > 0).astype(F32)
        r0, r1, c0, c1 = block_bounds(s, info)
        m = pair_dot(overlap(row, 1.0, r0, r1).astype(BF16), overlap(col, 1.0, c0, c1).astype(BF16))
        for j in range(s.width // LN):
            out[j] = m[: s.rows, tiles(j)] * via


def finish_kernel(s, f, c, cu, up, down, *refs):
    parts, (u_out, defect_out, v, u, defect, sem) = refs[: s.nd], refs[s.nd :]
    d, _ = place()
    nj, n = s.j0 - 1, s.width // LN
    for step, part in enumerate(parts):
        e = lax.rem(d + s.nd - step, s.nd)
        for j in range(nj):
            for k in range(s.lz + 2):
                at = (k * nj + j) * s.rows
                v[k, e * nj + j, HY : HY + s.rows, :] = part[at : at + s.rows, :]
            for a in range(s.lz):
                at = (s.lz + 2) * nj * s.rows + (a * nj + j) * 2
                v[a + 1, e * nj + j, HY - 1 : HY, :] = part[at : at + 1, :]
                v[a + 1, e * nj + j, HY + s.rows : HY + s.rows + 1, :] = part[at + 1 : at + 2, :]
    lane = iota((8, LN), 1)
    first, last = lane == 0, lane == LN - 1
    zero = jnp.zeros((8, LN), F32)
    copies = []
    for a in range(s.lz):
        z = d * s.lz + a
        cz, above = c[z], cu[z] * c[z]
        if a > 0:
            below = cu[z - 1] * c[z - 1]
        for r in range(0, s.rows, 8):
            rows, own = slice(HY + r, HY + r + 8), slice(r, r + 8)
            x = [v[a + 1, j, rows, :] for j in range(n)]
            ahead = [pltpu.roll(w, LN - 1, 1) for w in x] + [zero]
            behind = [pltpu.roll(w, 1, 1) for w in x] + [zero]
            for j in range(n):
                k_up = above if a < s.lz - 1 else up[j, own, :]
                k_down = below if a > 0 else down[j, own, :]
                side = jnp.where(last, ahead[j + 1], ahead[j]) + jnp.where(first, behind[j - 1], behind[j])
                side += v[a + 1, j, HY + r - 1 : HY + r + 7, :] + v[a + 1, j, HY + r + 1 : HY + r + 9, :]
                g = cz * side + (k_up * v[a + 2, j, rows, :] + k_down * v[a, j, rows, :])
                u[a, own, tiles(j)] = x[j]
                defect[a, own, tiles(j)] = (f[a, own, tiles(j)] + g) - (4.0 * cz + k_up + k_down) * x[j]
        for k, (src, dst) in enumerate(((u, u_out), (defect, defect_out))):
            copies.append(pltpu.make_async_copy(src.at[a], dst.at[a], sem.at[2 * a + k]))
            copies[-1].start()
    for x in copies:
        x.wait()


def call(kernel, s, outs, scratch=(), to_hbm=False, from_hbm=False, in_vmem=False, limit=32 << 20):
    shapes = [pltpu.VMEM(o, F32) if in_vmem else jax.ShapeDtypeStruct(o, F32) for o in outs]
    spaces = [pl.BlockSpec(memory_space=m) for m in (pltpu.VMEM, pltpu.HBM)]

    def run(*args):
        total = sum(int(np.prod(a.shape)) * 4 for a in args) + sum(int(np.prod(o)) * 4 for o in outs)
        return pl.pallas_call(
            functools.partial(kernel, s),
            out_shape=shapes,
            in_specs=[spaces[from_hbm]] * len(args),
            out_specs=[spaces[to_hbm]] * len(outs),
            scratch_shapes=[pltpu.VMEM(x, F32) if isinstance(x, tuple) else x for x in scratch],
            compiler_params=pltpu.CompilerParams(vmem_limit_bytes=limit),
            cost_estimate=pl.CostEstimate(flops=4 * total, bytes_accessed=total, transcendentals=0),
        )(*args)

    return run


def shift(x, axis, by):
    n = lax.axis_size(axis)
    return lax.ppermute(x, axis, [(i, (i + by) % n) for i in range(n)])


def swap(x, odd):
    n = lax.axis_size("tile")
    to = [((k - odd) ^ 1) + odd for k in range(n)]
    return lax.ppermute(x, "tile", [(k, q if 0 <= q < n else k) for k, q in enumerate(to)])


def tables(s):
    p = np.arange(s.we)
    at = p // 4 + np.where(p >= s.wc + HX, s.w1 - s.we // 4, 0)
    down = at[:, None] == np.arange(s.w1)[None, :]
    q = np.arange(s.w1)
    k = q // 4 + np.where(q >= s.w1 - HX // 4, LN - s.w1 // 4, 0)
    used = (q < s.c1 + HX // 4) | (q >= s.w1 - HX // 4)
    spread2 = (np.arange(LN)[:, None] == k[None, :]) & used[None, :]
    r = np.arange(LN)
    down2 = (r // 4)[:, None] == (r % s.c2)[None, :]
    return [jnp.asarray(m, BF16) for m in (down.T, spread2, down2 * 0.25)]


def local(s, source_heating, material_thermal_values, layer_material, via_conductance, via_blocks):
    spread1, spread2, down2 = tables(s)
    down = pl.pallas_call(
        functools.partial(down_kernel, s),
        name="down",
        out_shape=jax.ShapeDtypeStruct((s.we, s.w1), BF16),
        compiler_params=pltpu.CompilerParams(vmem_limit_bytes=4 << 20),
        cost_estimate=pl.CostEstimate(flops=1 << 20, bytes_accessed=1 << 20, transcendentals=0),
    )()
    smem, packed = pltpu.SMEM, (s.part + 8, LN)
    sends = call(
        pack_kernel, s, [packed] * s.nd,
        [
            smem(material_thermal_values.shape, F32), smem(layer_material.shape, jnp.int32),
            smem((1, 1), F32), pltpu.VMEM((4, s.nb), jnp.int32),
            pltpu.VMEM(source_heating.shape, F32), pltpu.SemaphoreType.DMA((5,)),
        ],
        from_hbm=True, in_vmem=True, limit=VMEM - 4 * s.nd * packed[0] * packed[1],
    )(material_thermal_values, layer_material, via_conductance[None], via_blocks[0].T, source_heating)
    parts = [sends[0]] + [shift(sends[k], "die", k) for k in range(1, s.nd)]
    half = (s.nz * s.j0, HY, LN)
    one, two, prm = call(assemble_kernel, s, [half, half, (s.nd, 8, LN)])(*parts)
    f0, f1, small = (s.j0, s.re, LN), (s.j1, s.e1, LN), (s.nz, s.j1, s.r1, LN)
    fine, fine_v = (s.nz, *f0), (s.nz + 2, *f0)
    mid, mid_v = (s.nz, *f1), (s.nz + 2, *f1)
    slab, table = (s.nd * s.lz, s.nt, LN), (s.nz, 8, LN)
    up0, down0, e0, c, ic, cu, cd = call(
        coeff_fine_kernel, s, [(s.nd, *f0), (s.nd, *f0), fine, table, table, table, table]
    )(prm)
    flat, rbuf = (s.nz, s.r1, s.we), (s.nz * s.j0 * s.re, LN)
    from_two = swap(two, 1)
    from_one = swap(one, 0)
    f, v2, r1 = call(fine_first_kernel, s, [fine, fine_v, small], [fine_v, rbuf, flat])(
        from_one, from_two, one, two, up0, down0, e0, ic, cu, cd, down
    )
    up1, down1, e1, u2, l2, e2 = call(coeff_coarse_kernel, s, [(s.nd, *f1), (s.nd, *f1), mid, slab, slab, slab])(prm)

    def middle_first(r1):
        return call(
            middle_first_kernel, s,
            [mid, mid_v, (s.nd * s.nt * s.lz, LN)], [mid_v, (s.nz * 8, LN)],
        )(swap(r1, 0), r1, swap(r1, 1), up1, down1, e1, cu, cd, down2)

    def everywhere(send):
        return lax.all_to_all(send, ("die", "tile"), 0, 0, tiled=True)

    spaces = [(s.nd * s.lz, s.nt + 2 * HY, LN), (s.nz * 8, LN), (s.nz, 8, s.w1), mid_v, mid_v]
    spaces += [fine_v, fine_v, flat]
    rx, w2, send = middle_first(r1)
    levels = (u2, l2, e2, up1, down1, e1, up0, down0, e0)
    v, r1 = call(back_kernel, s, [fine_v, small], spaces + [rbuf])(
        everywhere(send), v2, f, w2, rx, *levels, cu, cd, spread2, spread1, down
    )
    rx, w2, send = middle_first(r1)
    piece = ((s.lz + 2) * (s.j0 - 1) * s.rows + 2 * s.lz * (s.j0 - 1), LN)
    sends = call(last_kernel, s, [piece] * s.nd, spaces)(
        everywhere(send), w2, rx, v, f, *levels, cu, cd, spread2, spread1
    )
    parts = [sends[0]] + [shift(sends[k], "die", k) for k in range(1, s.nd)]
    whole, columns = (s.lz, s.rows, s.width), (s.width // LN, s.rows, LN)
    own_up, own_down = call(coeff_own_kernel, s, [columns] * 2)(prm)
    scratch = [(s.lz + 2, s.width // LN, s.re, LN), whole, whole, pltpu.SemaphoreType.DMA((2 * s.lz,))]
    return tuple(call(finish_kernel, s, [whole] * 2, scratch, True)(source_heating, c, cu, own_up, own_down, *parts))


def solution(mesh):
    in_specs = (P("die", "tile", None), P(), P("die"), P("die"), P("die", None, None))
    out_specs = (P("die", "tile", None), P("die", "tile", None))

    def body(f, mat, material, conductance, blocks):
        s = Sizes(mesh.shape, f.shape, blocks.shape[1])
        return local(s, f, mat, material, conductance, blocks)

    return jax.shard_map(body, mesh=mesh, in_specs=in_specs, out_specs=out_specs, check_vma=False)
```

profile of v0, /device:TPU:1, one launch (start us, length us, event | category | flops | bytes accessed | tf_op | source)
XLA Modules:
  0.0 86.7 jit_solution(12220832136210341506)
XLA Ops:
  1.3 1.2 %shard_map.95 = (f32[328,128]{1,0:T(8,128)S(1)}, f32[328,128]{1,0:T(8,128)S(1)}, f32[328,128]{1,0:T(8,128)S(1)}, f32[328,128]{1,0:T(8,128)S(1)}) custom-call(f32[6]{0:T(128)} %mat_h.1, s32[4]{0:T(128)} %material_h.1, f32[1,1]{1,0:T(1,128)} %bitcast.8.conductance_h, s32[4,24]{1,0:T(4,128)} %bitcast.13, f32[4,16,2048]{2,1,0:T(8,128)} %f.1), custom_call_target="tpu_custom_call" | custom-call | flops 4785840 | bytes 1196460 | tf_op jit(solution)/shard_map/pallas_call | solution.py:587
  2.5 2.1 %collective-permute-start = (f32[328,128]{1,0:T(8,128)S(1)}, f32[328,128]{1,0:T(8,128)S(1)}, u32[]{:S(2)}, u32[]{:S(2)}) collective-permute-start(f32[328,128]{1,0:T(8,128)S(1)} %get-tuple-element.40), channel_id=1, source_target_pairs={{0,8},{8,16},{16,24},{24,0},{1,9},{9,17},{17,25},{25,1},{2,10},{10... | collective-permute-start | bytes 503816 | tf_op jit(solution)/shard_map/ppermute | solution.py:602
  4.6 1.2 %collective-permute-start.1 = (f32[328,128]{1,0:T(8,128)S(1)}, f32[328,128]{1,0:T(8,128)S(1)}, u32[]{:S(2)}, u32[]{:S(2)}) collective-permute-start(f32[328,128]{1,0:T(8,128)S(1)} %get-tuple-element.41), channel_id=1, source_target_pairs={{0,16},{8,24},{16,0},{24,8},{1,17},{9,25},{17,1},{25,9},{2,18},{10... | collective-permute-start | bytes 503816 | tf_op jit(solution)/shard_map/ppermute | solution.py:602
  5.8 1.2 %collective-permute-start.2 = (f32[328,128]{1,0:T(8,128)S(1)}, f32[328,128]{1,0:T(8,128)S(1)}, u32[]{:S(2)}, u32[]{:S(2)}) collective-permute-start(f32[328,128]{1,0:T(8,128)S(1)} %get-tuple-element.42), channel_id=1, source_target_pairs={{0,24},{8,0},{16,8},{24,16},{1,25},{9,1},{17,9},{25,17},{2,26},{10... | collective-permute-start | bytes 503816 | tf_op jit(solution)/shard_map/ppermute | solution.py:602
  7.0 2.6 %collective-permute-done.refs_1_ = f32[328,128]{1,0:T(8,128)S(1)} collective-permute-done((f32[328,128]{1,0:T(8,128)S(1)}, f32[328,128]{1,0:T(8,128)S(1)}, u32[]{:S(2)}, u32[]{:S(2)}) %collective-permute-start) | collective-permute-done | bytes 167968 | tf_op jit(solution)/shard_map/ppermute | solution.py:602
  9.5 4.3 %collective-permute-done.1.refs_2_ = f32[328,128]{1,0:T(8,128)S(1)} collective-permute-done((f32[328,128]{1,0:T(8,128)S(1)}, f32[328,128]{1,0:T(8,128)S(1)}, u32[]{:S(2)}, u32[]{:S(2)}) %collective-permute-start.1) | collective-permute-done | bytes 167968 | tf_op jit(solution)/shard_map/ppermute | solution.py:602
  13.9 0.0 collective-permute-done.2.refs_3_
  13.9 0.1 shard_map.96
  13.9 0.8 collective-permute-start.3
  14.8 3.1 %collective-permute-start.4 = (f32[80,8,128]{2,1,0:T(8,128)S(1)}, f32[80,8,128]{2,1,0:T(8,128)S(1)}, u32[]{:S(2)}, u32[]{:S(2)}) collective-permute-start(f32[80,8,128]{2,1,0:T(8,128)S(1)} %get-tuple-element.49.two), channel_id=1, source_target_pairs={{0,0},{1,2},{2,1},{3,4},{4,3},{5,6},{6,5},{7,7},{8,8},{9,10},{10,9... | collective-permute-start | bytes 983048 | tf_op jit(solution)/shard_map/ppermute | solution.py:608
  17.9 0.1 down.1
  18.0 0.8 shard_map.97
  18.8 0.0 collective-permute-done.3.from_one
  18.8 4.4 %collective-permute-done.4.from_two = f32[80,8,128]{2,1,0:T(8,128)S(1)} collective-permute-done((f32[80,8,128]{2,1,0:T(8,128)S(1)}, f32[80,8,128]{2,1,0:T(8,128)S(1)}, u32[]{:S(2)}, u32[]{:S(2)}) %collective-permute-start.4) | collective-permute-done | bytes 327712 | tf_op jit(solution)/shard_map/ppermute | solution.py:608
  23.2 0.0 copy-start.3
  23.2 0.0 copy-start.1
  23.2 0.0 copy-start.2
  23.2 2.6 %shard_map.99 = (f32[16,5,32,128]{3,2,1,0:T(8,128)S(1)}, f32[18,5,32,128]{3,2,1,0:T(8,128)S(1)}, f32[16,2,8,128]{3,2,1,0:T(8,128)S(1)}) custom-call(f32[80,8,128]{2,1,0:T(8,128)S(1)} %collective-permute-done.3.from_one, f32[80,8,128]{2,1,0:T(8,128)S(1)} %collective-permute-done.4.from_two, f32[80,8,128]{2,1,0:T(8,128)S(1)} %get-tuple-element.48.one, ...), custom_call_target="tpu_custom_call" | custom-call | flops 28180480 | bytes 7045120 | tf_op jit(solution)/shard_map/pallas_call | solution.py:587
  25.8 0.1 collective-permute-start.5
  25.9 3.6 %collective-permute-start.6 = (f32[16,2,8,128]{3,2,1,0:T(8,128)S(1)}, f32[16,2,8,128]{3,2,1,0:T(8,128)S(1)}, u32[]{:S(2)}, u32[]{:S(2)}) collective-permute-start(f32[16,2,8,128]{3,2,1,0:T(8,128)S(1)} %get-tuple-element.55.r1), channel_id=1, source_target_pairs={{0,0},{1,2},{2,1},{3,4},{4,3},{5,6},{6,5},{7,7},{8,8},{9,10},{10,9... | collective-permute-start | bytes 393224 | tf_op jit(solution)/shard_map/ppermute | solution.py:608
  29.5 0.6 shard_map.100
  30.0 0.0 collective-permute-done.5.r1a
  30.1 2.1 %collective-permute-done.6.r1b = f32[16,2,8,128]{3,2,1,0:T(8,128)S(1)} collective-permute-done((f32[16,2,8,128]{3,2,1,0:T(8,128)S(1)}, f32[16,2,8,128]{3,2,1,0:T(8,128)S(1)}, u32[]{:S(2)}, u32[]{:S(2)}) %collective-permute-start.6) | collective-permute-done | bytes 131104 | tf_op jit(solution)/shard_map/ppermute | solution.py:608
  32.2 0.0 copy-done.3
  32.2 1.1 %shard_map.101 = (f32[16,2,16,128]{3,2,1,0:T(8,128)S(1)}, f32[18,2,16,128]{3,2,1,0:T(8,128)S(1)}, f32[128,128]{1,0:T(8,128)S(1)}) custom-call(f32[16,2,8,128]{3,2,1,0:T(8,128)S(1)} %collective-permute-done.5.r1a, f32[16,2,8,128]{3,2,1,0:T(8,128)S(1)} %get-tuple-element.55.r1, f32[16,2,8,128]{3,2,1,0:T(8,128)S(1)} %collective-permute-done.6.r1b, ...), custom_call_target="tpu_custom_call" | custom-call | flops 6422528 | bytes 1605632 | tf_op jit(solution)/shard_map/pallas_call | solution.py:587
  33.3 11.9 %all_to_all.22 = f32[32,4,128]{2,1,0:T(4,128)S(1)} all-to-all(f32[32,4,128]{2,1,0:T(4,128)S(1)} %bitcast.12), channel_id=1, replica_groups=mesh['die'=4,'tile'=8] {'die','tile'}, dimensions={0} | all-to-all | bytes 131072 | tf_op jit(solution)/shard_map/all_to_all | solution.py:668
  45.2 0.0 copy-done.1
  45.2 0.0 copy-done.2
  45.2 7.7 %shard_map.102 = (f32[18,5,32,128]{3,2,1,0:T(8,128)S(1)}, f32[16,2,8,128]{3,2,1,0:T(8,128)S(1)}) custom-call(f32[128,128]{1,0:T(8,128)S(1)} %bitcast.10, f32[18,5,32,128]{3,2,1,0:T(8,128)S(1)} %get-tuple-element.60.v2, f32[16,5,32,128]{3,2,1,0:T(8,128)S(1)} %get-tuple-element.61.f, f32[18,2,16,128]{3,2,1,0:T(8,128)S(1)} %get-tuple-element.62.w2, ...), custom_call_target="tpu_custom_call" | custom-call | flops 36569088 | bytes 9142272 | tf_op jit(solution)/shard_map/pallas_call | solution.py:587
  52.9 0.5 collective-permute-start.7
  53.4 2.1 %collective-permute-start.8 = (f32[16,2,8,128]{3,2,1,0:T(8,128)S(1)}, f32[16,2,8,128]{3,2,1,0:T(8,128)S(1)}, u32[]{:S(2)}, u32[]{:S(2)}) collective-permute-start(f32[16,2,8,128]{3,2,1,0:T(8,128)S(1)} %get-tuple-element.67.r1), channel_id=1, source_target_pairs={{0,0},{1,2},{2,1},{3,4},{4,3},{5,6},{6,5},{7,7},{8,8},{9,10},{10,9... | collective-permute-start | bytes 393224 | tf_op jit(solution)/shard_map/ppermute | solution.py:608
  55.5 0.0 collective-permute-done.7.r1a
  55.5 4.2 %collective-permute-done.8.r1b = f32[16,2,8,128]{3,2,1,0:T(8,128)S(1)} collective-permute-done((f32[16,2,8,128]{3,2,1,0:T(8,128)S(1)}, f32[16,2,8,128]{3,2,1,0:T(8,128)S(1)}, u32[]{:S(2)}, u32[]{:S(2)}) %collective-permute-start.8) | collective-permute-done | bytes 131104 | tf_op jit(solution)/shard_map/ppermute | solution.py:608
  59.7 1.1 %shard_map.103 = (f32[16,2,16,128]{3,2,1,0:T(8,128)S(1)}, f32[18,2,16,128]{3,2,1,0:T(8,128)S(1)}, f32[128,128]{1,0:T(8,128)S(1)}) custom-call(f32[16,2,8,128]{3,2,1,0:T(8,128)S(1)} %collective-permute-done.7.r1a, f32[16,2,8,128]{3,2,1,0:T(8,128)S(1)} %get-tuple-element.67.r1, f32[16,2,8,128]{3,2,1,0:T(8,128)S(1)} %collective-permute-done.8.r1b, ...), custom_call_target="tpu_custom_call" | custom-call | flops 6422528 | bytes 1605632 | tf_op jit(solution)/shard_map/pallas_call | solution.py:587
  60.7 8.1 %all_to_all.23 = f32[32,4,128]{2,1,0:T(4,128)S(1)} all-to-all(f32[32,4,128]{2,1,0:T(4,128)S(1)} %bitcast.11), channel_id=1, replica_groups=mesh['die'=4,'tile'=8] {'die','tile'}, dimensions={0} | all-to-all | bytes 131072 | tf_op jit(solution)/shard_map/all_to_all | solution.py:668
  68.9 0.0 copy-start
  68.9 4.5 %shard_map.104 = (f32[416,128]{1,0:T(8,128)S(1)}, f32[416,128]{1,0:T(8,128)S(1)}, f32[416,128]{1,0:T(8,128)S(1)}, f32[416,128]{1,0:T(8,128)S(1)}) custom-call(f32[128,128]{1,0:T(8,128)S(1)} %bitcast.9, f32[18,2,16,128]{3,2,1,0:T(8,128)S(1)} %get-tuple-element.69.w2, f32[16,2,16,128]{3,2,1,0:T(8,128)S(1)} %get-tuple-element.70.rx, ...), custom_call_target="tpu_custom_call" | custom-call | flops 30932992 | bytes 7733248 | tf_op jit(solution)/shard_map/pallas_call | solution.py:587
  73.4 0.3 collective-permute-start.10
  73.7 1.0 %collective-permute-start.11 = (f32[416,128]{1,0:T(8,128)S(1)}, f32[416,128]{1,0:T(8,128)S(1)}, u32[]{:S(2)}, u32[]{:S(2)}) collective-permute-start(f32[416,128]{1,0:T(8,128)S(1)} %get-tuple-element.75), channel_id=1, source_target_pairs={{0,24},{8,0},{16,8},{24,16},{1,25},{9,1},{17,9},{25,17},{2,26},{10... | collective-permute-start | bytes 638984 | tf_op jit(solution)/shard_map/ppermute | solution.py:602
  74.7 0.5 collective-permute-start.9
  75.2 0.6 shard_map.98
  75.8 4.1 %collective-permute-done.10.refs_2_ = f32[416,128]{1,0:T(8,128)S(1)} collective-permute-done((f32[416,128]{1,0:T(8,128)S(1)}, f32[416,128]{1,0:T(8,128)S(1)}, u32[]{:S(2)}, u32[]{:S(2)}) %collective-permute-start.10) | collective-permute-done | bytes 213024 | tf_op jit(solution)/shard_map/ppermute | solution.py:602
  79.9 0.0 collective-permute-done.11.refs_3_
  79.9 5.5 %collective-permute-done.9.refs_1_ = f32[416,128]{1,0:T(8,128)S(1)} collective-permute-done((f32[416,128]{1,0:T(8,128)S(1)}, f32[416,128]{1,0:T(8,128)S(1)}, u32[]{:S(2)}, u32[]{:S(2)}) %collective-permute-start.9) | collective-permute-done | bytes 213024 | tf_op jit(solution)/shard_map/ppermute | solution.py:602
  85.3 0.0 copy-done
  85.3 1.3 %shard_map.105 = (f32[4,16,2048]{2,1,0:T(8,128)}, f32[4,16,2048]{2,1,0:T(8,128)}) custom-call(f32[4,16,2048]{2,1,0:T(8,128)S(1)} %copy-done, f32[16,8,128]{2,1,0:T(8,128)S(1)} %get-tuple-element.44.c, f32[16,8,128]{2,1,0:T(8,128)S(1)} %get-tuple-element.45.cu, f32[16,16,128]{2,1,0:T(8,128)S(1)} %get-tuple-element.46.up, ...), custom_call_target="tpu_custom_call" | custom-call | flops 11272192 | bytes 2818048 | tf_op jit(solution)/shard_map/pallas_call | solution.py:587
Async XLA Ops:
  2.5 7.1 %collective-permute-start = (f32[328,128]{1,0:T(8,128)S(1)}, f32[328,128]{1,0:T(8,128)S(1)}, u32[]{:S(2)}, u32[]{:S(2)}) collective-permute-start(f32[328,128]{1,0:T(8,128)S(1)} %get-tuple-element.40), channel_id=1, source_target_pairs={{0,8},{8,16},{16,24},{24,0},{1,9},{9,17},{17,25},{25,1},{2,10},{10... | collective-permute-start | bytes 503816 | tf_op jit(solution)/shard_map/ppermute | solution.py:602
  4.6 9.3 %collective-permute-start.1 = (f32[328,128]{1,0:T(8,128)S(1)}, f32[328,128]{1,0:T(8,128)S(1)}, u32[]{:S(2)}, u32[]{:S(2)}) collective-permute-start(f32[328,128]{1,0:T(8,128)S(1)} %get-tuple-element.41), channel_id=1, source_target_pairs={{0,16},{8,24},{16,0},{24,8},{1,17},{9,25},{17,1},{25,9},{2,18},{10... | collective-permute-start | bytes 503816 | tf_op jit(solution)/shard_map/ppermute | solution.py:602
  5.8 8.1 %collective-permute-start.2 = (f32[328,128]{1,0:T(8,128)S(1)}, f32[328,128]{1,0:T(8,128)S(1)}, u32[]{:S(2)}, u32[]{:S(2)}) collective-permute-start(f32[328,128]{1,0:T(8,128)S(1)} %get-tuple-element.42), channel_id=1, source_target_pairs={{0,24},{8,0},{16,8},{24,16},{1,25},{9,1},{17,9},{25,17},{2,26},{10... | collective-permute-start | bytes 503816 | tf_op jit(solution)/shard_map/ppermute | solution.py:602
  13.9 4.9 %collective-permute-start.3 = (f32[80,8,128]{2,1,0:T(8,128)S(1)}, f32[80,8,128]{2,1,0:T(8,128)S(1)}, u32[]{:S(2)}, u32[]{:S(2)}) collective-permute-start(f32[80,8,128]{2,1,0:T(8,128)S(1)} %get-tuple-element.48.one), channel_id=1, source_target_pairs={{0,1},{1,0},{2,3},{3,2},{4,5},{5,4},{6,7},{7,6},{8,9},{9,8},{10,11... | collective-permute-start | bytes 983048 | tf_op jit(solution)/shard_map/ppermute | solution.py:608
  14.8 8.4 %collective-permute-start.4 = (f32[80,8,128]{2,1,0:T(8,128)S(1)}, f32[80,8,128]{2,1,0:T(8,128)S(1)}, u32[]{:S(2)}, u32[]{:S(2)}) collective-permute-start(f32[80,8,128]{2,1,0:T(8,128)S(1)} %get-tuple-element.49.two), channel_id=1, source_target_pairs={{0,0},{1,2},{2,1},{3,4},{4,3},{5,6},{6,5},{7,7},{8,8},{9,10},{10,9... | collective-permute-start | bytes 983048 | tf_op jit(solution)/shard_map/ppermute | solution.py:608
  23.2 9.0 %copy-start.3 = (bf16[128,128]{1,0:T(8,128)(2,1)S(1)}, bf16[128,128]{1,0:T(8,128)(2,1)}, u32[]{:S(2)}) copy-start(bf16[128,128]{1,0:T(8,128)(2,1)} %constant.8.clone.down2) | copy-start | bytes 98308
  23.2 22.0 %copy-start.1 = (bf16[256,640]{1,0:T(8,128)(2,1)S(1)}, bf16[256,640]{1,0:T(8,128)(2,1)}, u32[]{:S(2)}) copy-start(bf16[256,640]{1,0:T(8,128)(2,1)} %constant.6.clone.spread1) | copy-start | bytes 983044
  23.2 22.0 %copy-start.2 = (bf16[128,256]{1,0:T(8,128)(2,1)S(1)}, bf16[128,256]{1,0:T(8,128)(2,1)}, u32[]{:S(2)}) copy-start(bf16[128,256]{1,0:T(8,128)(2,1)} %constant.7.clone.spread2) | copy-start | bytes 196612
  25.8 4.2 %collective-permute-start.5 = (f32[16,2,8,128]{3,2,1,0:T(8,128)S(1)}, f32[16,2,8,128]{3,2,1,0:T(8,128)S(1)}, u32[]{:S(2)}, u32[]{:S(2)}) collective-permute-start(f32[16,2,8,128]{3,2,1,0:T(8,128)S(1)} %get-tuple-element.55.r1), channel_id=1, source_target_pairs={{0,1},{1,0},{2,3},{3,2},{4,5},{5,4},{6,7},{7,6},{8,9},{9,8},{10,11... | collective-permute-start | bytes 393224 | tf_op jit(solution)/shard_map/ppermute | solution.py:608
  25.9 6.3 %collective-permute-start.6 = (f32[16,2,8,128]{3,2,1,0:T(8,128)S(1)}, f32[16,2,8,128]{3,2,1,0:T(8,128)S(1)}, u32[]{:S(2)}, u32[]{:S(2)}) collective-permute-start(f32[16,2,8,128]{3,2,1,0:T(8,128)S(1)} %get-tuple-element.55.r1), channel_id=1, source_target_pairs={{0,0},{1,2},{2,1},{3,4},{4,3},{5,6},{6,5},{7,7},{8,8},{9,10},{10,9... | collective-permute-start | bytes 393224 | tf_op jit(solution)/shard_map/ppermute | solution.py:608
  52.9 2.5 %collective-permute-start.7 = (f32[16,2,8,128]{3,2,1,0:T(8,128)S(1)}, f32[16,2,8,128]{3,2,1,0:T(8,128)S(1)}, u32[]{:S(2)}, u32[]{:S(2)}) collective-permute-start(f32[16,2,8,128]{3,2,1,0:T(8,128)S(1)} %get-tuple-element.67.r1), channel_id=1, source_target_pairs={{0,1},{1,0},{2,3},{3,2},{4,5},{5,4},{6,7},{7,6},{8,9},{9,8},{10,11... | collective-permute-start | bytes 393224 | tf_op jit(solution)/shard_map/ppermute | solution.py:608
  53.4 6.3 %collective-permute-start.8 = (f32[16,2,8,128]{3,2,1,0:T(8,128)S(1)}, f32[16,2,8,128]{3,2,1,0:T(8,128)S(1)}, u32[]{:S(2)}, u32[]{:S(2)}) collective-permute-start(f32[16,2,8,128]{3,2,1,0:T(8,128)S(1)} %get-tuple-element.67.r1), channel_id=1, source_target_pairs={{0,0},{1,2},{2,1},{3,4},{4,3},{5,6},{6,5},{7,7},{8,8},{9,10},{10,9... | collective-permute-start | bytes 393224 | tf_op jit(solution)/shard_map/ppermute | solution.py:608
  68.9 16.5 %copy-start = (f32[4,16,2048]{2,1,0:T(8,128)S(1)}, f32[4,16,2048]{2,1,0:T(8,128)}, u32[]{:S(2)}) copy-start(f32[4,16,2048]{2,1,0:T(8,128)} %f.1) | copy-start | bytes 1572868
  73.4 6.5 %collective-permute-start.10 = (f32[416,128]{1,0:T(8,128)S(1)}, f32[416,128]{1,0:T(8,128)S(1)}, u32[]{:S(2)}, u32[]{:S(2)}) collective-permute-start(f32[416,128]{1,0:T(8,128)S(1)} %get-tuple-element.74), channel_id=1, source_target_pairs={{0,16},{8,24},{16,0},{24,8},{1,17},{9,25},{17,1},{25,9},{2,18},{10... | collective-permute-start | bytes 638984 | tf_op jit(solution)/shard_map/ppermute | solution.py:602
  73.7 6.2 %collective-permute-start.11 = (f32[416,128]{1,0:T(8,128)S(1)}, f32[416,128]{1,0:T(8,128)S(1)}, u32[]{:S(2)}, u32[]{:S(2)}) collective-permute-start(f32[416,128]{1,0:T(8,128)S(1)} %get-tuple-element.75), channel_id=1, source_target_pairs={{0,24},{8,0},{16,8},{24,16},{1,25},{9,1},{17,9},{25,17},{2,26},{10... | collective-permute-start | bytes 638984 | tf_op jit(solution)/shard_map/ppermute | solution.py:602
  74.7 10.7 %collective-permute-start.9 = (f32[416,128]{1,0:T(8,128)S(1)}, f32[416,128]{1,0:T(8,128)S(1)}, u32[]{:S(2)}, u32[]{:S(2)}) collective-permute-start(f32[416,128]{1,0:T(8,128)S(1)} %get-tuple-element.73), channel_id=1, source_target_pairs={{0,8},{8,16},{16,24},{24,0},{1,9},{9,17},{17,25},{25,1},{2,10},{10... | collective-permute-start | bytes 638984 | tf_op jit(solution)/shard_map/ppermute | solution.py:602
where the time goes:
time: 88.4 us; the launch traced here: 86.7 us
  waiting for transfers between devices  27.1 us (31%)
  Pallas kernels  21.7 us (25%)
  blocking collectives  20.1 us (23%)
  starting transfers between devices  16.4 us (19%)
  between operations  1.41 us (2%)
    pallas_call x11, Pallas kernels, run(): pl.pallas_call(functools.partial(kernel, s), out_shape=shapes, in_specs=[...  21.6 us
    all_to_all x2, blocking collectives, everywhere(): return lax.all_to_all(send, ('die', 'tile'), 0, 0, tiled=True)  20.1 us
    ppermute x6, waiting for transfers between devices, shift(): return lax.ppermute(x, axis, [(i, (i + by) % n) for i in range(n)])  16.5 us
    ppermute x6, waiting for transfers between devices, swap(): lax.ppermute(x, 'tile', [(k, q if 0 <= q < n else k) for k, q in enumerat...  10.7 us
    ppermute x6, starting transfers between devices, swap(): lax.ppermute(x, 'tile', [(k, q if 0 <= q < n else k) for k, q in enumerat...  10.1 us
    ppermute x6, starting transfers between devices, shift(): return lax.ppermute(x, axis, [(i, (i + by) % n) for i in range(n)])  6.25 us
  transfers between devices with their start and end apart: 12, of which 7 were waited for; matrix products, arithmetic and copies ran while one was open for 0% of the time, Pallas kernels for 2%

commit v1 on v0

--- a/solution.py
+++ b/solution.py
@@ -212,36 +212,21 @@
     values = die_values(s, prm)
     cond, vert, via, blocks = values
     level_coeffs(s, 1, values, up1, down1, e1)
-    group = iota((1, LN), 1) // s.c2
-    xin = iota((1, LN), 1) % s.c2
-
-    def by_group(values):
-        out = jnp.zeros((1, LN), F32)
-        for g in range(s.nd):
-            out = jnp.where(group == g, values[g], out)
-        return out
-
-    cl = [by_group([cond[s.lz * g + a] for g in range(s.nd)]) * 16.0 for a in range(s.lz)]
-    vl = [by_group([vert[s.lz * g + a] for g in range(s.nd)]) * 256.0 for a in range(s.lz)]
-    vial = by_group(via)
-    row2 = (iota((1, LN), 1) * 16).astype(F32)
-    ra = jnp.concatenate([overlap(row2, 16.0, b[0], b[1]) for b in blocks], axis=0).astype(BF16)
-    zero2 = jnp.zeros((s.nt, LN), F32)
-    for e in range(s.nd):
-        col2 = ((e * s.c2 + xin) * 16).astype(F32)
-        cb = jnp.concatenate(
-            [jnp.where(group == g, overlap(col2, 16.0, b[2], b[3]), 0.0) for g, b in enumerate(blocks)],
-            axis=0,
-        ).astype(BF16)
-        v2 = pair_dot(ra, cb)[: s.nt] * vial
-        ups = [zero2 + vl[a] for a in range(s.lz - 1)] + [v2]
-        first = jnp.where(iota((s.nt, LN), 1) >= s.c2, pltpu.roll(v2, s.c2, 1), 0.0)
-        lows = [first] + ups[:-1]
-        for a in range(s.lz):
-            q = e * s.lz + a
-            u2[q] = ups[a] / cl[a]
-            l2[q] = lows[a] / cl[a]
-            e2[q] = OMEGA * cl[a] / (4.0 * cl[a] + ups[a] + lows[a])
+    at = (iota((1, LN), 1) * 16).astype(F32)
+    ups = []
+    for z in range(s.nz):
+        g = z // s.lz
+        if z % s.lz < s.lz - 1:
+            up = jnp.zeros((s.nt, LN), F32) + vert[z] * 256.0
+        else:
+            r0, r1, c0, c1 = blocks[g]
+            up = pair_dot(overlap(at, 16.0, r0, r1).astype(BF16), overlap(at, 16.0, c0, c1).astype(BF16))
+            up = up[: s.nt] * via[g]
+        down = ups[-1] if ups else jnp.zeros((s.nt, LN), F32)
+        ups.append(up)
+        u2[z] = up / (cond[z] * 16.0)
+        l2[z] = down / (cond[z] * 16.0)
+        e2[z] = OMEGA * 16.0 * cond[z] / (64.0 * cond[z] + up + down)
 
 
 class Level:
@@ -294,7 +279,11 @@
         b[s.nz + 1] = jnp.zeros(b.shape[1:], F32)
 
 
-def restrict(s, level, src, f, lo, hi, down, rbuf, sums, r1):
+def turn(a):
+    return a * 2 * (HX // 4) + HX // 4
+
+
+def restrict(s, level, src, f, lo, hi, down, rbuf, sums, r1, ship):
     for k in range(s.nz * s.j0):
         rbuf[k * s.re : k * s.re + 8, :] = jnp.zeros((8, LN), F32)
         rbuf[(k + 1) * s.re - 8 : (k + 1) * s.re, :] = jnp.zeros((8, LN), F32)
@@ -312,9 +301,17 @@
 
     lax.fori_loop(0, s.nz, body, 0)
     out = split_dot(sums[...].reshape(s.nz * s.r1, s.we), down[...])
-    for z in range(s.nz):
-        for j in range(s.j1):
-            r1[z, j] = out[z * s.r1 : (z + 1) * s.r1, tiles(j)]
+    part = iota((s.r1, LN), 1) // (HX // 2)
+    for g in range(s.nd):
+        shared = jnp.zeros((s.r1, LN), F32)
+        for a in range(s.lz):
+            z = g * s.lz + a
+            x, halo = (out[z * s.r1 : (z + 1) * s.r1, tiles(j)] for j in range(s.j1))
+            r1[z, 0] = x
+            r1[z, 1] = halo
+            ship[z] = x
+            shared = jnp.where(part == a, pltpu.roll(halo, turn(a), 1), shared)
+        ship[s.nz + g] = shared
 
 
 def down_kernel(s, out):
@@ -323,7 +320,7 @@
     out[...] = jnp.where(at == q, 0.25, 0.0).astype(BF16)
 
 
-def fine_first_kernel(s, from_one, from_two, one, two, up0, down0, e0, ic, cu, cd, down, f, v2, r1, va, rbuf, sums):
+def fine_first_kernel(s, from_one, from_two, one, two, up0, down0, e0, ic, cu, cd, down, f, v2, r1, ship, va, rbuf, sums):
     level = Level(s, 0, up0, down0, e0, cu, cd)
     lower = even()
     zero_ends(s, va, v2)
@@ -340,7 +337,7 @@
 
     lax.fori_loop(0, s.nz, body, 0)
     level.sweep(va, v2, f, 1, s.re - 1)
-    restrict(s, level, v2, f, HY - 4, s.re - HY + 4, down, rbuf, sums, r1)
+    restrict(s, level, v2, f, HY - 4, s.re - HY + 4, down, rbuf, sums, r1, ship)
 
 
 def middle_first_kernel(s, r1a, r1, r1b, up1, down1, e1, cu, cd, down2, rx, w2, send, wa, buf):
@@ -350,18 +347,24 @@
     lower = even()
     zero_ends(s, wa, w2)
 
-    def body(z, carry):
-        for j in range(s.j1):
-            mid = pltpu.roll(r1[z, j], half // 2, 0)
-            up = jnp.where(sub >= pad, mid, jnp.where(lower, r1b[z, j], r1a[z, j]))
-            down = jnp.where(sub < own - (half - pad), mid, jnp.where(lower, r1a[z, j], r1b[z, j]))
-            rx[z, j, :half, :] = up
-            rx[z, j, half:, :] = down
-            wa[z + 1, j, :half, :] = e1[z, j, :half, :] * up
-            wa[z + 1, j, half:, :] = e1[z, j, half:, :] * down
+    def body(g, carry):
+        for a in range(s.lz):
+            z = g * s.lz + a
+            for j in range(s.j1):
+                mid = pltpu.roll(r1[z, j], half // 2, 0)
+                if j == 0:
+                    p, q = r1a[z], r1b[z]
+                else:
+                    p, q = (pltpu.roll(x[s.nz + g], LN - turn(a), 1) for x in (r1a, r1b))
+                up = jnp.where(sub >= pad, mid, jnp.where(lower, q, p))
+                down = jnp.where(sub < own - (half - pad), mid, jnp.where(lower, p, q))
+                rx[z, j, :half, :] = up
+                rx[z, j, half:, :] = down
+                wa[z + 1, j, :half, :] = e1[z, j, :half, :] * up
+                wa[z + 1, j, half:, :] = e1[z, j, half:, :] * down
         return carry
 
-    lax.fori_loop(0, s.nz, body, 0)
+    lax.fori_loop(0, s.nd, body, 0)
     level.sweep(wa, w2, rx, pad - 4, pad + own + 4)
 
     def put(z, j, rows, x):
@@ -381,65 +384,47 @@
 
 
 def coarse(s, got, u2, l2, e2, cs):
-    lane = iota((s.nt, LN), 1)
-    x, t = lane % s.c2, iota((s.nt, LN), 0)
-    first_x, last_x = x == 0, x == s.c2 - 1
-    slabs = s.nd * s.lz
+    lane, t = iota((s.nt, LN), 1), iota((s.nt, LN), 0)
     rhs, v = [], []
-    for q in range(slabs):
-        e, a = q // s.lz, q % s.lz
-        r = got[pl.ds(e * s.nt * s.lz + a, s.nt, stride=s.lz), :]
+    for z in range(s.nz):
+        g, a = z // s.lz, z % s.lz
+        r = jnp.zeros((s.nt, LN), F32)
+        for e in range(s.nd):
+            x = got[pl.ds(e * s.nt * s.lz + a, s.nt, stride=s.lz), :]
+            x = pltpu.roll(x, (e - g) * s.c2 % LN, 1) if e != g else x
+            r = jnp.where(lane // s.c2 == e, x, r)
         rhs.append(r)
-        v.append(e2[q] * r)
-    zero = jnp.zeros((s.nt, LN), F32)
+        v.append(e2[z] * r)
 
     def body(_, v):
         new = []
-        for q in range(slabs):
-            e, a = q // s.lz, q % s.lz
-            w = v[q]
-            right = pltpu.roll(v[q + s.lz], s.c2 - 1, 1) if e < s.nd - 1 else zero
-            left = pltpu.roll(v[q - s.lz], LN - (s.c2 - 1), 1) if e > 0 else zero
-            side = jnp.where(last_x, right, pltpu.roll(w, LN - 1, 1))
-            side += jnp.where(first_x, left, pltpu.roll(w, 1, 1))
+        for z in range(s.nz):
+            w = v[z]
+            side = jnp.where(lane == LN - 1, 0.0, pltpu.roll(w, LN - 1, 1))
+            side += jnp.where(lane == 0, 0.0, pltpu.roll(w, 1, 1))
             side += jnp.where(t == s.nt - 1, 0.0, pltpu.roll(w, s.nt - 1, 0))
             side += jnp.where(t == 0, 0.0, pltpu.roll(w, 1, 0))
-            if a < s.lz - 1:
-                up = v[q + 1]
-            else:
-                up = jnp.where(lane >= LN - s.c2, 0.0, pltpu.roll(v[q - a], LN - s.c2, 1))
-            if a > 0:
-                down = v[q - 1]
-            else:
-                down = jnp.where(lane < s.c2, 0.0, pltpu.roll(v[q + s.lz - 1], s.c2, 1))
-            g = (rhs[q] + side) + (u2[q] * up + l2[q] * down)
-            new.append((1.0 - OMEGA) * w + e2[q] * g)
+            g = rhs[z] + side
+            if z < s.nz - 1:
+                g += u2[z] * v[z + 1]
+            if z > 0:
+                g += l2[z] * v[z - 1]
+            new.append((1.0 - OMEGA) * w + e2[z] * g)
         return tuple(new)
 
     v = lax.fori_loop(0, NC - 1, body, tuple(v))
-    for q in range(slabs):
-        cs[q, :HY, :] = jnp.zeros((HY, LN), F32)
-        cs[q, HY + s.nt :, :] = jnp.zeros((HY, LN), F32)
-        cs[q, HY : HY + s.nt, :] = v[q]
+    for z in range(s.nz):
+        cs[z, :HY, :] = jnp.zeros((HY, LN), F32)
+        cs[z, HY + s.nt :, :] = jnp.zeros((HY, LN), F32)
+        cs[z, HY : HY + s.nt, :] = v[z]
 
 
 def middle_last(s, level, cs, spread2, w2, rx, comp, wide, wa, wb):
     d, t = place()
-    lane, upper = iota((8, LN), 1), iota((8, LN), 0) < 4
-    after = lax.rem(d + 1, s.nd) * s.lz
-    before = lax.rem(d + s.nd - 1, s.nd) * s.lz
+    upper = iota((8, LN), 0) < 4
     zero_ends(s, wa, wb)
-    for a in range(s.lz):
-        rows = [cs[base + a, pl.ds(HY - 1 + t, 8), :] for base in (d * s.lz, after, before)]
-        for g in range(s.nd):
-            turn = []
-            for r, by in zip(rows, (0, s.c2, LN - s.c2)):
-                by = (by - g * s.c2) % LN
-                turn.append(pltpu.roll(r, by, 1) if by else r)
-            z = g * s.lz + a
-            comp[8 * z : 8 * z + 8, :] = jnp.where(
-                lane < s.c2, turn[0], jnp.where(lane < LN // 2, turn[1], turn[2])
-            )
+    for z in range(s.nz):
+        comp[8 * z : 8 * z + 8, :] = pltpu.roll(cs[z, pl.ds(HY - 1 + t, 8), :], lax.rem(LN - d * s.c2, LN), 1)
     wide[...] = split_dot(comp[...], spread2[...]).reshape(wide.shape)
 
     def body(z, carry):
@@ -476,7 +461,7 @@
 def back_kernel(
     s, got, v2, f, w2, rx,
     u2, l2, e2, up1, down1, e1, up0, down0, e0, cu, cd, spread2, spread1, down,
-    v, r1, cs, comp, wide2, wa, wb, va, vb, wide, rbuf,
+    v, r1, ship, cs, comp, wide2, wa, wb, va, vb, wide, rbuf,
 ):
     fine = Level(s, 0, up0, down0, e0, cu, cd)
     middle = Level(s, 1, up1, down1, e1, cu, cd)
@@ -488,7 +473,7 @@
     fine.sweep(vb, va, f, 3, s.re - 3)
     fine.sweep(va, vb, f, 4, s.re - 4)
     fine.sweep(vb, v, f, 5, s.re - 5)
-    restrict(s, fine, v, f, HY, HY + s.rows, down, rbuf, wide, r1)
+    restrict(s, fine, v, f, HY, HY + s.rows, down, rbuf, wide, r1, ship)
 
 
 def last_kernel(
@@ -650,31 +635,32 @@
     up0, down0, e0, c, ic, cu, cd = call(
         coeff_fine_kernel, s, [(s.nd, *f0), (s.nd, *f0), fine, table, table, table, table]
     )(prm)
+    shared = (s.nz + s.nd, s.r1, LN)
     flat, rbuf = (s.nz, s.r1, s.we), (s.nz * s.j0 * s.re, LN)
     from_two = swap(two, 1)
     from_one = swap(one, 0)
-    f, v2, r1 = call(fine_first_kernel, s, [fine, fine_v, small], [fine_v, rbuf, flat])(
+    f, v2, r1, ship = call(fine_first_kernel, s, [fine, fine_v, small, shared], [fine_v, rbuf, flat])(
         from_one, from_two, one, two, up0, down0, e0, ic, cu, cd, down
     )
     up1, down1, e1, u2, l2, e2 = call(coeff_coarse_kernel, s, [(s.nd, *f1), (s.nd, *f1), mid, slab, slab, slab])(prm)
 
-    def middle_first(r1):
+    def middle_first(r1, ship):
         return call(
             middle_first_kernel, s,
             [mid, mid_v, (s.nd * s.nt * s.lz, LN)], [mid_v, (s.nz * 8, LN)],
-        )(swap(r1, 0), r1, swap(r1, 1), up1, down1, e1, cu, cd, down2)
+        )(swap(ship, 0), r1, swap(ship, 1), up1, down1, e1, cu, cd, down2)
 
     def everywhere(send):
         return lax.all_to_all(send, ("die", "tile"), 0, 0, tiled=True)
 
     spaces = [(s.nd * s.lz, s.nt + 2 * HY, LN), (s.nz * 8, LN), (s.nz, 8, s.w1), mid_v, mid_v]
     spaces += [fine_v, fine_v, flat]
-    rx, w2, send = middle_first(r1)
+    rx, w2, send = middle_first(r1, ship)
     levels = (u2, l2, e2, up1, down1, e1, up0, down0, e0)
-    v, r1 = call(back_kernel, s, [fine_v, small], spaces + [rbuf])(
+    v, r1, ship = call(back_kernel, s, [fine_v, small, shared], spaces + [rbuf])(
         everywhere(send), v2, f, w2, rx, *levels, cu, cd, spread2, spread1, down
     )
-    rx, w2, send = middle_first(r1)
+    rx, w2, send = middle_first(r1, ship)
     piece = ((s.lz + 2) * (s.j0 - 1) * s.rows + 2 * s.lz * (s.j0 - 1), LN)
     sends = call(last_kernel, s, [piece] * s.nd, spaces)(
         everywhere(send), w2, rx, v, f, *levels, cu, cd, spread2, spread1

time: 88.4 us -> 87.7 us (level)
  waiting for transfers between devices: 27.1 us -> 26.1 us
    ppermute x6, waiting for transfers between devices: 10.7 us -> 9.68 us  [swap(): lax.ppermute(x, 'tile', [(k, q if 0 <= q < n else k) for k, q in enumerat...]
where the time goes in v1:
time: 87.7 us; the launch traced here: 86 us
  waiting for transfers between devices  26.1 us (30%)
  Pallas kernels  22 us (25%)
  blocking collectives  20.1 us (23%)
  starting transfers between devices  16.4 us (19%)
  between operations  1.41 us (2%)
    pallas_call x11, Pallas kernels, run(): pl.pallas_call(functools.partial(kernel, s), out_shape=shapes, in_specs=[...  21.9 us
    all_to_all x2, blocking collectives, everywhere(): return lax.all_to_all(send, ('die', 'tile'), 0, 0, tiled=True)  20.1 us
    ppermute x6, waiting for transfers between devices, shift(): return lax.ppermute(x, axis, [(i, (i + by) % n) for i in range(n)])  16.4 us
    ppermute x6, starting transfers between devices, swap(): lax.ppermute(x, 'tile', [(k, q if 0 <= q < n else k) for k, q in enumerat...  10.1 us
    ppermute x6, waiting for transfers between devices, swap(): lax.ppermute(x, 'tile', [(k, q if 0 <= q < n else k) for k, q in enumerat...  9.68 us
    ppermute x6, starting transfers between devices, shift(): return lax.ppermute(x, axis, [(i, (i + by) % n) for i in range(n)])  6.26 us
  transfers between devices with their start and end apart: 12, of which 7 were waited for; matrix products, arithmetic and copies ran while one was open for 0% of the time, Pallas kernels for 2%

profile of v1, /device:TPU:1, one launch (start us, length us, event | category | flops | bytes accessed | tf_op | source)
XLA Modules:
  0.0 86.0 jit_solution(4029007716721177973)
XLA Ops:
  1.3 1.2 %shard_map.95 = (f32[328,128]{1,0:T(8,128)S(1)}, f32[328,128]{1,0:T(8,128)S(1)}, f32[328,128]{1,0:T(8,128)S(1)}, f32[328,128]{1,0:T(8,128)S(1)}) custom-call(f32[6]{0:T(128)} %mat_h.1, s32[4]{0:T(128)} %material_h.1, f32[1,1]{1,0:T(1,128)} %bitcast.8.conductance_h, s32[4,24]{1,0:T(4,128)} %bitcast.13, f32[4,16,2048]{2,1,0:T(8,128)} %f.1), custom_call_target="tpu_custom_call" | custom-call | flops 4785840 | bytes 1196460 | tf_op jit(solution)/shard_map/pallas_call | solution.py:572
  2.5 2.1 %collective-permute-start = (f32[328,128]{1,0:T(8,128)S(1)}, f32[328,128]{1,0:T(8,128)S(1)}, u32[]{:S(2)}, u32[]{:S(2)}) collective-permute-start(f32[328,128]{1,0:T(8,128)S(1)} %get-tuple-element.42), channel_id=1, source_target_pairs={{0,8},{8,16},{16,24},{24,0},{1,9},{9,17},{17,25},{25,1},{2,10},{10... | collective-permute-start | bytes 503816 | tf_op jit(solution)/shard_map/ppermute | solution.py:587
  4.6 1.2 %collective-permute-start.1 = (f32[328,128]{1,0:T(8,128)S(1)}, f32[328,128]{1,0:T(8,128)S(1)}, u32[]{:S(2)}, u32[]{:S(2)}) collective-permute-start(f32[328,128]{1,0:T(8,128)S(1)} %get-tuple-element.43), channel_id=1, source_target_pairs={{0,16},{8,24},{16,0},{24,8},{1,17},{9,25},{17,1},{25,9},{2,18},{10... | collective-permute-start | bytes 503816 | tf_op jit(solution)/shard_map/ppermute | solution.py:587
  5.8 1.2 %collective-permute-start.2 = (f32[328,128]{1,0:T(8,128)S(1)}, f32[328,128]{1,0:T(8,128)S(1)}, u32[]{:S(2)}, u32[]{:S(2)}) collective-permute-start(f32[328,128]{1,0:T(8,128)S(1)} %get-tuple-element.44), channel_id=1, source_target_pairs={{0,24},{8,0},{16,8},{24,16},{1,25},{9,1},{17,9},{25,17},{2,26},{10... | collective-permute-start | bytes 503816 | tf_op jit(solution)/shard_map/ppermute | solution.py:587
  7.0 2.6 %collective-permute-done.refs_1_ = f32[328,128]{1,0:T(8,128)S(1)} collective-permute-done((f32[328,128]{1,0:T(8,128)S(1)}, f32[328,128]{1,0:T(8,128)S(1)}, u32[]{:S(2)}, u32[]{:S(2)}) %collective-permute-start) | collective-permute-done | bytes 167968 | tf_op jit(solution)/shard_map/ppermute | solution.py:587
  9.5 4.3 %collective-permute-done.1.refs_2_ = f32[328,128]{1,0:T(8,128)S(1)} collective-permute-done((f32[328,128]{1,0:T(8,128)S(1)}, f32[328,128]{1,0:T(8,128)S(1)}, u32[]{:S(2)}, u32[]{:S(2)}) %collective-permute-start.1) | collective-permute-done | bytes 167968 | tf_op jit(solution)/shard_map/ppermute | solution.py:587
  13.9 0.0 collective-permute-done.2.refs_3_
  13.9 0.1 shard_map.96
  13.9 0.8 collective-permute-start.3
  14.8 3.1 %collective-permute-start.4 = (f32[80,8,128]{2,1,0:T(8,128)S(1)}, f32[80,8,128]{2,1,0:T(8,128)S(1)}, u32[]{:S(2)}, u32[]{:S(2)}) collective-permute-start(f32[80,8,128]{2,1,0:T(8,128)S(1)} %get-tuple-element.51.two), channel_id=1, source_target_pairs={{0,0},{1,2},{2,1},{3,4},{4,3},{5,6},{6,5},{7,7},{8,8},{9,10},{10,9... | collective-permute-start | bytes 983048 | tf_op jit(solution)/shard_map/ppermute | solution.py:593
  17.9 0.1 down.1
  18.0 0.8 shard_map.97
  18.8 0.0 collective-permute-done.3.from_one
  18.8 4.4 %collective-permute-done.4.from_two = f32[80,8,128]{2,1,0:T(8,128)S(1)} collective-permute-done((f32[80,8,128]{2,1,0:T(8,128)S(1)}, f32[80,8,128]{2,1,0:T(8,128)S(1)}, u32[]{:S(2)}, u32[]{:S(2)}) %collective-permute-start.4) | collective-permute-done | bytes 327712 | tf_op jit(solution)/shard_map/ppermute | solution.py:593
  23.2 0.0 copy-start.3
  23.2 0.0 copy-start.1
  23.2 0.0 copy-start.2
  23.2 2.7 %shard_map.99 = (f32[16,5,32,128]{3,2,1,0:T(8,128)S(1)}, f32[18,5,32,128]{3,2,1,0:T(8,128)S(1)}, f32[16,2,8,128]{3,2,1,0:T(8,128)S(1)}, f32[20,8,128]{2,1,0:T(8,128)S(1)}) custom-call(f32[80,8,128]{2,1,0:T(8,128)S(1)} %collective-permute-done.3.from_one, f32[80,8,128]{2,1,0:T(8,128)S(1)} %collective-permute-done.4.from_two, ...), custom_call_target="tpu_custom_call" | custom-call | flops 28508160 | bytes 7127040 | tf_op jit(solution)/shard_map/pallas_call | solution.py:572
  25.9 0.1 collective-permute-start.5
  26.0 3.6 %collective-permute-start.6 = (f32[20,8,128]{2,1,0:T(8,128)S(1)}, f32[20,8,128]{2,1,0:T(8,128)S(1)}, u32[]{:S(2)}, u32[]{:S(2)}) collective-permute-start(f32[20,8,128]{2,1,0:T(8,128)S(1)} %get-tuple-element.57), channel_id=1, source_target_pairs={{0,0},{1,2},{2,1},{3,4},{4,3},{5,6},{6,5},{7,7},{8,8},{9,10},{10,9... | collective-permute-start | bytes 245768 | tf_op jit(solution)/shard_map/ppermute | solution.py:593
  29.5 0.5 shard_map.100
  30.1 0.0 collective-permute-done.5.r1a
  30.1 1.7 %collective-permute-done.6.r1b = f32[20,8,128]{2,1,0:T(8,128)S(1)} collective-permute-done((f32[20,8,128]{2,1,0:T(8,128)S(1)}, f32[20,8,128]{2,1,0:T(8,128)S(1)}, u32[]{:S(2)}, u32[]{:S(2)}) %collective-permute-start.6) | collective-permute-done | bytes 81952 | tf_op jit(solution)/shard_map/ppermute | solution.py:593
  31.7 0.0 copy-done.3
  31.7 1.3 %shard_map.101 = (f32[16,2,16,128]{3,2,1,0:T(8,128)S(1)}, f32[18,2,16,128]{3,2,1,0:T(8,128)S(1)}, f32[128,128]{1,0:T(8,128)S(1)}) custom-call(f32[20,8,128]{2,1,0:T(8,128)S(1)} %collective-permute-done.5.r1a, f32[16,2,8,128]{3,2,1,0:T(8,128)S(1)} %get-tuple-element.58.r1, f32[20,8,128]{2,1,0:T(8,128)S(1)} %collective-permute-done.6.r1b, ...), custom_call_target="tpu_custom_call" | custom-call | flops 6029312 | bytes 1507328 | tf_op jit(solution)/shard_map/pallas_call | solution.py:572
  33.0 11.9 %all_to_all.22 = f32[32,4,128]{2,1,0:T(4,128)S(1)} all-to-all(f32[32,4,128]{2,1,0:T(4,128)S(1)} %bitcast.12), channel_id=1, replica_groups=mesh['die'=4,'tile'=8] {'die','tile'}, dimensions={0} | all-to-all | bytes 131072 | tf_op jit(solution)/shard_map/all_to_all | solution.py:654
  44.9 0.0 copy-done.1
  44.9 0.0 copy-done.2
  44.9 7.7 %shard_map.102 = (f32[18,5,32,128]{3,2,1,0:T(8,128)S(1)}, f32[16,2,8,128]{3,2,1,0:T(8,128)S(1)}, f32[20,8,128]{2,1,0:T(8,128)S(1)}) custom-call(f32[128,128]{1,0:T(8,128)S(1)} %bitcast.10, f32[18,5,32,128]{3,2,1,0:T(8,128)S(1)} %get-tuple-element.63.v2, f32[16,5,32,128]{3,2,1,0:T(8,128)S(1)} %get-tuple-element.64.f, ...), custom_call_target="tpu_custom_call" | custom-call | flops 36896768 | bytes 9224192 | tf_op jit(solution)/shard_map/pallas_call | solution.py:572
  52.6 0.5 collective-permute-start.7
  53.1 2.1 %collective-permute-start.8 = (f32[20,8,128]{2,1,0:T(8,128)S(1)}, f32[20,8,128]{2,1,0:T(8,128)S(1)}, u32[]{:S(2)}, u32[]{:S(2)}) collective-permute-start(f32[20,8,128]{2,1,0:T(8,128)S(1)} %get-tuple-element.70), channel_id=1, source_target_pairs={{0,0},{1,2},{2,1},{3,4},{4,3},{5,6},{6,5},{7,7},{8,8},{9,10},{10,9... | collective-permute-start | bytes 245768 | tf_op jit(solution)/shard_map/ppermute | solution.py:593
  55.2 0.0 collective-permute-done.7.r1a
  55.2 3.7 %collective-permute-done.8.r1b = f32[20,8,128]{2,1,0:T(8,128)S(1)} collective-permute-done((f32[20,8,128]{2,1,0:T(8,128)S(1)}, f32[20,8,128]{2,1,0:T(8,128)S(1)}, u32[]{:S(2)}, u32[]{:S(2)}) %collective-permute-start.8) | collective-permute-done | bytes 81952 | tf_op jit(solution)/shard_map/ppermute | solution.py:593
  58.9 1.3 %shard_map.103 = (f32[16,2,16,128]{3,2,1,0:T(8,128)S(1)}, f32[18,2,16,128]{3,2,1,0:T(8,128)S(1)}, f32[128,128]{1,0:T(8,128)S(1)}) custom-call(f32[20,8,128]{2,1,0:T(8,128)S(1)} %collective-permute-done.7.r1a, f32[16,2,8,128]{3,2,1,0:T(8,128)S(1)} %get-tuple-element.71.r1, f32[20,8,128]{2,1,0:T(8,128)S(1)} %collective-permute-done.8.r1b, ...), custom_call_target="tpu_custom_call" | custom-call | flops 6029312 | bytes 1507328 | tf_op jit(solution)/shard_map/pallas_call | solution.py:572
  60.1 8.1 %all_to_all.23 = f32[32,4,128]{2,1,0:T(4,128)S(1)} all-to-all(f32[32,4,128]{2,1,0:T(4,128)S(1)} %bitcast.11), channel_id=1, replica_groups=mesh['die'=4,'tile'=8] {'die','tile'}, dimensions={0} | all-to-all | bytes 131072 | tf_op jit(solution)/shard_map/all_to_all | solution.py:654
  68.2 0.0 copy-start
  68.2 4.5 %shard_map.104 = (f32[416,128]{1,0:T(8,128)S(1)}, f32[416,128]{1,0:T(8,128)S(1)}, f32[416,128]{1,0:T(8,128)S(1)}, f32[416,128]{1,0:T(8,128)S(1)}) custom-call(f32[128,128]{1,0:T(8,128)S(1)} %bitcast.9, f32[18,2,16,128]{3,2,1,0:T(8,128)S(1)} %get-tuple-element.73.w2, f32[16,2,16,128]{3,2,1,0:T(8,128)S(1)} %get-tuple-element.74.rx, ...), custom_call_target="tpu_custom_call" | custom-call | flops 30932992 | bytes 7733248 | tf_op jit(solution)/shard_map/pallas_call | solution.py:572
  72.7 0.3 collective-permute-start.10
  73.0 1.0 %collective-permute-start.11 = (f32[416,128]{1,0:T(8,128)S(1)}, f32[416,128]{1,0:T(8,128)S(1)}, u32[]{:S(2)}, u32[]{:S(2)}) collective-permute-start(f32[416,128]{1,0:T(8,128)S(1)} %get-tuple-element.79), channel_id=1, source_target_pairs={{0,24},{8,0},{16,8},{24,16},{1,25},{9,1},{17,9},{25,17},{2,26},{10... | collective-permute-start | bytes 638984 | tf_op jit(solution)/shard_map/ppermute | solution.py:587
  74.0 0.5 collective-permute-start.9
  74.5 0.6 shard_map.98
  75.1 4.1 %collective-permute-done.10.refs_2_ = f32[416,128]{1,0:T(8,128)S(1)} collective-permute-done((f32[416,128]{1,0:T(8,128)S(1)}, f32[416,128]{1,0:T(8,128)S(1)}, u32[]{:S(2)}, u32[]{:S(2)}) %collective-permute-start.10) | collective-permute-done | bytes 213024 | tf_op jit(solution)/shard_map/ppermute | solution.py:587
  79.2 0.0 collective-permute-done.11.refs_3_
  79.2 5.5 %collective-permute-done.9.refs_1_ = f32[416,128]{1,0:T(8,128)S(1)} collective-permute-done((f32[416,128]{1,0:T(8,128)S(1)}, f32[416,128]{1,0:T(8,128)S(1)}, u32[]{:S(2)}, u32[]{:S(2)}) %collective-permute-start.9) | collective-permute-done | bytes 213024 | tf_op jit(solution)/shard_map/ppermute | solution.py:587
  84.6 0.0 copy-done
  84.6 1.3 %shard_map.105 = (f32[4,16,2048]{2,1,0:T(8,128)}, f32[4,16,2048]{2,1,0:T(8,128)}) custom-call(f32[4,16,2048]{2,1,0:T(8,128)S(1)} %copy-done, f32[16,8,128]{2,1,0:T(8,128)S(1)} %get-tuple-element.46.c, f32[16,8,128]{2,1,0:T(8,128)S(1)} %get-tuple-element.47.cu, f32[16,16,128]{2,1,0:T(8,128)S(1)} %get-tuple-element.48.up, ...), custom_call_target="tpu_custom_call" | custom-call | flops 11272192 | bytes 2818048 | tf_op jit(solution)/shard_map/pallas_call | solution.py:572
Async XLA Ops:
  2.5 7.1 %collective-permute-start = (f32[328,128]{1,0:T(8,128)S(1)}, f32[328,128]{1,0:T(8,128)S(1)}, u32[]{:S(2)}, u32[]{:S(2)}) collective-permute-start(f32[328,128]{1,0:T(8,128)S(1)} %get-tuple-element.42), channel_id=1, source_target_pairs={{0,8},{8,16},{16,24},{24,0},{1,9},{9,17},{17,25},{25,1},{2,10},{10... | collective-permute-start | bytes 503816 | tf_op jit(solution)/shard_map/ppermute | solution.py:587
  4.6 9.3 %collective-permute-start.1 = (f32[328,128]{1,0:T(8,128)S(1)}, f32[328,128]{1,0:T(8,128)S(1)}, u32[]{:S(2)}, u32[]{:S(2)}) collective-permute-start(f32[328,128]{1,0:T(8,128)S(1)} %get-tuple-element.43), channel_id=1, source_target_pairs={{0,16},{8,24},{16,0},{24,8},{1,17},{9,25},{17,1},{25,9},{2,18},{10... | collective-permute-start | bytes 503816 | tf_op jit(solution)/shard_map/ppermute | solution.py:587
  5.8 8.1 %collective-permute-start.2 = (f32[328,128]{1,0:T(8,128)S(1)}, f32[328,128]{1,0:T(8,128)S(1)}, u32[]{:S(2)}, u32[]{:S(2)}) collective-permute-start(f32[328,128]{1,0:T(8,128)S(1)} %get-tuple-element.44), channel_id=1, source_target_pairs={{0,24},{8,0},{16,8},{24,16},{1,25},{9,1},{17,9},{25,17},{2,26},{10... | collective-permute-start | bytes 503816 | tf_op jit(solution)/shard_map/ppermute | solution.py:587
  13.9 4.9 %collective-permute-start.3 = (f32[80,8,128]{2,1,0:T(8,128)S(1)}, f32[80,8,128]{2,1,0:T(8,128)S(1)}, u32[]{:S(2)}, u32[]{:S(2)}) collective-permute-start(f32[80,8,128]{2,1,0:T(8,128)S(1)} %get-tuple-element.50.one), channel_id=1, source_target_pairs={{0,1},{1,0},{2,3},{3,2},{4,5},{5,4},{6,7},{7,6},{8,9},{9,8},{10,11... | collective-permute-start | bytes 983048 | tf_op jit(solution)/shard_map/ppermute | solution.py:593
  14.8 8.4 %collective-permute-start.4 = (f32[80,8,128]{2,1,0:T(8,128)S(1)}, f32[80,8,128]{2,1,0:T(8,128)S(1)}, u32[]{:S(2)}, u32[]{:S(2)}) collective-permute-start(f32[80,8,128]{2,1,0:T(8,128)S(1)} %get-tuple-element.51.two), channel_id=1, source_target_pairs={{0,0},{1,2},{2,1},{3,4},{4,3},{5,6},{6,5},{7,7},{8,8},{9,10},{10,9... | collective-permute-start | bytes 983048 | tf_op jit(solution)/shard_map/ppermute | solution.py:593
  23.2 8.6 %copy-start.3 = (bf16[128,128]{1,0:T(8,128)(2,1)S(1)}, bf16[128,128]{1,0:T(8,128)(2,1)}, u32[]{:S(2)}) copy-start(bf16[128,128]{1,0:T(8,128)(2,1)} %constant.8.clone.down2) | copy-start | bytes 98308
  23.2 21.8 %copy-start.1 = (bf16[256,640]{1,0:T(8,128)(2,1)S(1)}, bf16[256,640]{1,0:T(8,128)(2,1)}, u32[]{:S(2)}) copy-start(bf16[256,640]{1,0:T(8,128)(2,1)} %constant.6.clone.spread1) | copy-start | bytes 983044
  23.2 21.8 %copy-start.2 = (bf16[128,256]{1,0:T(8,128)(2,1)S(1)}, bf16[128,256]{1,0:T(8,128)(2,1)}, u32[]{:S(2)}) copy-start(bf16[128,256]{1,0:T(8,128)(2,1)} %constant.7.clone.spread2) | copy-start | bytes 196612
  25.9 4.2 %collective-permute-start.5 = (f32[20,8,128]{2,1,0:T(8,128)S(1)}, f32[20,8,128]{2,1,0:T(8,128)S(1)}, u32[]{:S(2)}, u32[]{:S(2)}) collective-permute-start(f32[20,8,128]{2,1,0:T(8,128)S(1)} %get-tuple-element.57), channel_id=1, source_target_pairs={{0,1},{1,0},{2,3},{3,2},{4,5},{5,4},{6,7},{7,6},{8,9},{9,8},{10,11... | collective-permute-start | bytes 245768 | tf_op jit(solution)/shard_map/ppermute | solution.py:593
  26.0 5.8 %collective-permute-start.6 = (f32[20,8,128]{2,1,0:T(8,128)S(1)}, f32[20,8,128]{2,1,0:T(8,128)S(1)}, u32[]{:S(2)}, u32[]{:S(2)}) collective-permute-start(f32[20,8,128]{2,1,0:T(8,128)S(1)} %get-tuple-element.57), channel_id=1, source_target_pairs={{0,0},{1,2},{2,1},{3,4},{4,3},{5,6},{6,5},{7,7},{8,8},{9,10},{10,9... | collective-permute-start | bytes 245768 | tf_op jit(solution)/shard_map/ppermute | solution.py:593
  52.6 2.5 %collective-permute-start.7 = (f32[20,8,128]{2,1,0:T(8,128)S(1)}, f32[20,8,128]{2,1,0:T(8,128)S(1)}, u32[]{:S(2)}, u32[]{:S(2)}) collective-permute-start(f32[20,8,128]{2,1,0:T(8,128)S(1)} %get-tuple-element.70), channel_id=1, source_target_pairs={{0,1},{1,0},{2,3},{3,2},{4,5},{5,4},{6,7},{7,6},{8,9},{9,8},{10,11... | collective-permute-start | bytes 245768 | tf_op jit(solution)/shard_map/ppermute | solution.py:593
  53.1 5.7 %collective-permute-start.8 = (f32[20,8,128]{2,1,0:T(8,128)S(1)}, f32[20,8,128]{2,1,0:T(8,128)S(1)}, u32[]{:S(2)}, u32[]{:S(2)}) collective-permute-start(f32[20,8,128]{2,1,0:T(8,128)S(1)} %get-tuple-element.70), channel_id=1, source_target_pairs={{0,0},{1,2},{2,1},{3,4},{4,3},{5,6},{6,5},{7,7},{8,8},{9,10},{10,9... | collective-permute-start | bytes 245768 | tf_op jit(solution)/shard_map/ppermute | solution.py:593
  68.2 16.4 %copy-start = (f32[4,16,2048]{2,1,0:T(8,128)S(1)}, f32[4,16,2048]{2,1,0:T(8,128)}, u32[]{:S(2)}) copy-start(f32[4,16,2048]{2,1,0:T(8,128)} %f.1) | copy-start | bytes 1572868
  72.7 6.5 %collective-permute-start.10 = (f32[416,128]{1,0:T(8,128)S(1)}, f32[416,128]{1,0:T(8,128)S(1)}, u32[]{:S(2)}, u32[]{:S(2)}) collective-permute-start(f32[416,128]{1,0:T(8,128)S(1)} %get-tuple-element.78), channel_id=1, source_target_pairs={{0,16},{8,24},{16,0},{24,8},{1,17},{9,25},{17,1},{25,9},{2,18},{10... | collective-permute-start | bytes 638984 | tf_op jit(solution)/shard_map/ppermute | solution.py:587
  73.0 6.2 %collective-permute-start.11 = (f32[416,128]{1,0:T(8,128)S(1)}, f32[416,128]{1,0:T(8,128)S(1)}, u32[]{:S(2)}, u32[]{:S(2)}) collective-permute-start(f32[416,128]{1,0:T(8,128)S(1)} %get-tuple-element.79), channel_id=1, source_target_pairs={{0,24},{8,0},{16,8},{24,16},{1,25},{9,1},{17,9},{25,17},{2,26},{10... | collective-permute-start | bytes 638984 | tf_op jit(solution)/shard_map/ppermute | solution.py:587
  74.0 10.7 %collective-permute-start.9 = (f32[416,128]{1,0:T(8,128)S(1)}, f32[416,128]{1,0:T(8,128)S(1)}, u32[]{:S(2)}, u32[]{:S(2)}) collective-permute-start(f32[416,128]{1,0:T(8,128)S(1)} %get-tuple-element.77), channel_id=1, source_target_pairs={{0,8},{8,16},{16,24},{24,0},{1,9},{9,17},{17,25},{25,1},{2,10},{10... | collective-permute-start | bytes 638984 | tf_op jit(solution)/shard_map/ppermute | solution.py:587

commit v2 on v1

--- a/solution.py
+++ b/solution.py
@@ -75,11 +75,12 @@
 
 def pack_kernel(s, mat_h, material_h, conductance_h, blocks_h, f_h, *refs):
     outs, (mat, material, conductance, blocks, f, sem) = refs[: s.nd], refs[s.nd :]
-    pairs = [(f_h, f), (mat_h, mat), (material_h, material), (conductance_h, conductance), (blocks_h, blocks)]
+    pairs = [(f_h.at[z], f.at[z]) for z in range(s.lz)]
+    pairs += [(mat_h, mat), (material_h, material), (conductance_h, conductance), (blocks_h, blocks)]
     copies = [pltpu.make_async_copy(a, b, sem.at[k]) for k, (a, b) in enumerate(pairs)]
     for c in copies:
         c.start()
-    for c in copies[1:]:
+    for c in copies[s.lz :]:
         c.wait()
     d, _ = place()
     lane, sub = iota((8, LN), 1), iota((8, LN), 0)
@@ -89,23 +90,20 @@
     for out in outs:
         out[s.part :, :] = info
         out[s.part : s.part + 4, : s.nb] = blocks[...].astype(F32)
-    copies[0].wait()
     low = iota((s.rows, LN), 1) < HX
-    for step, out in enumerate(outs):
-        e = lax.rem(d + step, s.nd)
-        right = lax.rem(e + 1, s.nd) * s.wc
-        left = lax.rem(e + s.nd - 1, s.nd) * s.wc + (s.wc - LN)
-
-        def column(z, at):
-            return f[z, :, pl.ds(pl.multiple_of(at, LN), LN)]
-
-        for z in range(s.lz):
+    for z in range(s.lz):
+        copies[z].wait()
+        for step, out in enumerate(outs):
+            e = lax.rem(d + step, s.nd)
+            right = lax.rem(e + 1, s.nd) * s.wc
+            left = lax.rem(e + s.nd - 1, s.nd) * s.wc + (s.wc - LN)
+            column = lambda at: f[z, :, pl.ds(pl.multiple_of(at, LN), LN)]
             for j in range(s.j0):
                 at = (z * s.j0 + j) * s.rows
                 if j < s.j0 - 1:
-                    x = column(z, e * s.wc + j * LN)
+                    x = column(e * s.wc + j * LN)
                 else:
-                    x = jnp.where(low, column(z, right), column(z, left))
+                    x = jnp.where(low, column(right), column(left))
                 out[at : at + s.rows, :] = x
 
 
@@ -258,7 +256,7 @@
                         emit(z, j, rows, v[j], x, k_up, k_down)
             return carry
 
-        lax.fori_loop(0, s.nd, group, 0)
+        lax.fori_loop(0, s.nd, group, 0, unroll=2)
 
     def sweep(self, src, dst, f, lo, hi):
         def emit(z, j, rows, v, g, *_):
@@ -621,7 +619,7 @@
         [
             smem(material_thermal_values.shape, F32), smem(layer_material.shape, jnp.int32),
             smem((1, 1), F32), pltpu.VMEM((4, s.nb), jnp.int32),
-            pltpu.VMEM(source_heating.shape, F32), pltpu.SemaphoreType.DMA((5,)),
+            pltpu.VMEM(source_heating.shape, F32), pltpu.SemaphoreType.DMA((s.lz + 4,)),
         ],
         from_hbm=True, in_vmem=True, limit=VMEM - 4 * s.nd * packed[0] * packed[1],
     )(material_thermal_values, layer_material, via_conductance[None], via_blocks[0].T, source_heating)

time: 87.7 us -> 85.3 us (0.973)
  the two profiles are of different devices: /device:TPU:1 before, /device:TPU:0 now
where the time goes in v2:
time: 85.3 us; the launch traced here: 85.1 us
  blocking collectives  29.4 us (34%)
  Pallas kernels  19.6 us (23%)
  starting transfers between devices  18.3 us (21%)
  waiting for transfers between devices  16.4 us (19%)
  between operations  1.42 us (2%)
    all_to_all x2, blocking collectives, everywhere(): return lax.all_to_all(send, ('die', 'tile'), 0, 0, tiled=True)  29.4 us
    pallas_call x11, Pallas kernels, run(): pl.pallas_call(functools.partial(kernel, s), out_shape=shapes, in_specs=[...  19.5 us
    ppermute x6, waiting for transfers between devices, shift(): return lax.ppermute(x, axis, [(i, (i + by) % n) for i in range(n)])  15.8 us
    ppermute x6, starting transfers between devices, swap(): lax.ppermute(x, 'tile', [(k, q if 0 <= q < n else k) for k, q in enumerat...  9.54 us
    ppermute x6, starting transfers between devices, shift(): return lax.ppermute(x, axis, [(i, (i + by) % n) for i in range(n)])  8.76 us
  transfers between devices with their start and end apart: 12, of which 7 were waited for; matrix products, arithmetic and copies ran while one was open for 0% of the time, Pallas kernels for 2%

profile of v2, /device:TPU:0, one launch (start us, length us, event | category | flops | bytes accessed | tf_op | source)
XLA Modules:
  0.0 85.1 jit_solution(4031712845416160140)
XLA Ops:
  1.3 1.2 %shard_map.95 = (f32[328,128]{1,0:T(8,128)S(1)}, f32[328,128]{1,0:T(8,128)S(1)}, f32[328,128]{1,0:T(8,128)S(1)}, f32[328,128]{1,0:T(8,128)S(1)}) custom-call(f32[6]{0:T(128)} %mat_h.1, s32[4]{0:T(128)} %material_h.1, f32[1,1]{1,0:T(1,128)} %bitcast.8.conductance_h, s32[4,24]{1,0:T(4,128)} %bitcast.13, f32[4,16,2048]{2,1,0:T(8,128)} %f.1), custom_call_target="tpu_custom_call" | custom-call | flops 4785840 | bytes 1196460 | tf_op jit(solution)/shard_map/pallas_call | solution.py:570
  2.5 3.0 %collective-permute-start = (f32[328,128]{1,0:T(8,128)S(1)}, f32[328,128]{1,0:T(8,128)S(1)}, u32[]{:S(2)}, u32[]{:S(2)}) collective-permute-start(f32[328,128]{1,0:T(8,128)S(1)} %get-tuple-element.42), channel_id=1, source_target_pairs={{0,8},{8,16},{16,24},{24,0},{1,9},{9,17},{17,25},{25,1},{2,10},{10... | collective-permute-start | bytes 503816 | tf_op jit(solution)/shard_map/ppermute | solution.py:585
  5.5 1.5 %collective-permute-start.1 = (f32[328,128]{1,0:T(8,128)S(1)}, f32[328,128]{1,0:T(8,128)S(1)}, u32[]{:S(2)}, u32[]{:S(2)}) collective-permute-start(f32[328,128]{1,0:T(8,128)S(1)} %get-tuple-element.43), channel_id=1, source_target_pairs={{0,16},{8,24},{16,0},{24,8},{1,17},{9,25},{17,1},{25,9},{2,18},{10... | collective-permute-start | bytes 503816 | tf_op jit(solution)/shard_map/ppermute | solution.py:585
  7.0 1.4 %collective-permute-start.2 = (f32[328,128]{1,0:T(8,128)S(1)}, f32[328,128]{1,0:T(8,128)S(1)}, u32[]{:S(2)}, u32[]{:S(2)}) collective-permute-start(f32[328,128]{1,0:T(8,128)S(1)} %get-tuple-element.44), channel_id=1, source_target_pairs={{0,24},{8,0},{16,8},{24,16},{1,25},{9,1},{17,9},{25,17},{2,26},{10... | collective-permute-start | bytes 503816 | tf_op jit(solution)/shard_map/ppermute | solution.py:585
  8.5 3.2 %collective-permute-done.refs_1_ = f32[328,128]{1,0:T(8,128)S(1)} collective-permute-done((f32[328,128]{1,0:T(8,128)S(1)}, f32[328,128]{1,0:T(8,128)S(1)}, u32[]{:S(2)}, u32[]{:S(2)}) %collective-permute-start) | collective-permute-done | bytes 167968 | tf_op jit(solution)/shard_map/ppermute | solution.py:585
  11.6 2.7 %collective-permute-done.1.refs_2_ = f32[328,128]{1,0:T(8,128)S(1)} collective-permute-done((f32[328,128]{1,0:T(8,128)S(1)}, f32[328,128]{1,0:T(8,128)S(1)}, u32[]{:S(2)}, u32[]{:S(2)}) %collective-permute-start.1) | collective-permute-done | bytes 167968 | tf_op jit(solution)/shard_map/ppermute | solution.py:585
  14.3 0.3 collective-permute-done.2.refs_3_
  14.6 0.1 shard_map.96
  14.7 0.1 collective-permute-start.3
  14.8 0.7 collective-permute-start.4
  15.5 0.1 down.1
  15.5 0.8 shard_map.97
  16.4 0.0 collective-permute-done.3.from_one
  16.4 0.0 collective-permute-done.4.from_two
  16.4 0.0 copy-start.3
  16.4 0.0 copy-start.1
  16.4 0.0 copy-start.2
  16.4 2.5 %shard_map.99 = (f32[16,5,32,128]{3,2,1,0:T(8,128)S(1)}, f32[18,5,32,128]{3,2,1,0:T(8,128)S(1)}, f32[16,2,8,128]{3,2,1,0:T(8,128)S(1)}, f32[20,8,128]{2,1,0:T(8,128)S(1)}) custom-call(f32[80,8,128]{2,1,0:T(8,128)S(1)} %collective-permute-done.3.from_one, f32[80,8,128]{2,1,0:T(8,128)S(1)} %collective-permute-done.4.from_two, ...), custom_call_target="tpu_custom_call" | custom-call | flops 28508160 | bytes 7127040 | tf_op jit(solution)/shard_map/pallas_call | solution.py:570
  18.9 7.3 %collective-permute-start.5 = (f32[20,8,128]{2,1,0:T(8,128)S(1)}, f32[20,8,128]{2,1,0:T(8,128)S(1)}, u32[]{:S(2)}, u32[]{:S(2)}) collective-permute-start(f32[20,8,128]{2,1,0:T(8,128)S(1)} %get-tuple-element.57), channel_id=1, source_target_pairs={{0,1},{1,0},{2,3},{3,2},{4,5},{5,4},{6,7},{7,6},{8,9},{9,8},{10,11... | collective-permute-start | bytes 245768 | tf_op jit(solution)/shard_map/ppermute | solution.py:591
  26.2 0.7 collective-permute-start.6
  26.8 0.5 shard_map.100
  27.4 0.0 collective-permute-done.5.r1a
  27.4 0.0 collective-permute-done.6.r1b
  27.4 0.0 copy-done.3
  27.4 1.0 %shard_map.101 = (f32[16,2,16,128]{3,2,1,0:T(8,128)S(1)}, f32[18,2,16,128]{3,2,1,0:T(8,128)S(1)}, f32[128,128]{1,0:T(8,128)S(1)}) custom-call(f32[20,8,128]{2,1,0:T(8,128)S(1)} %collective-permute-done.5.r1a, f32[16,2,8,128]{3,2,1,0:T(8,128)S(1)} %get-tuple-element.58.r1, f32[20,8,128]{2,1,0:T(8,128)S(1)} %collective-permute-done.6.r1b, ...), custom_call_target="tpu_custom_call" | custom-call | flops 6029312 | bytes 1507328 | tf_op jit(solution)/shard_map/pallas_call | solution.py:570
  28.4 16.4 %all_to_all.22 = f32[32,4,128]{2,1,0:T(4,128)S(1)} all-to-all(f32[32,4,128]{2,1,0:T(4,128)S(1)} %bitcast.12), channel_id=1, replica_groups=mesh['die'=4,'tile'=8] {'die','tile'}, dimensions={0} | all-to-all | bytes 131072 | tf_op jit(solution)/shard_map/all_to_all | solution.py:652
  44.7 0.0 copy-done.1
  44.7 0.0 copy-done.2
  44.8 6.7 %shard_map.102 = (f32[18,5,32,128]{3,2,1,0:T(8,128)S(1)}, f32[16,2,8,128]{3,2,1,0:T(8,128)S(1)}, f32[20,8,128]{2,1,0:T(8,128)S(1)}) custom-call(f32[128,128]{1,0:T(8,128)S(1)} %bitcast.10, f32[18,5,32,128]{3,2,1,0:T(8,128)S(1)} %get-tuple-element.63.v2, f32[16,5,32,128]{3,2,1,0:T(8,128)S(1)} %get-tuple-element.64.f, ...), custom_call_target="tpu_custom_call" | custom-call | flops 36896768 | bytes 9224192 | tf_op jit(solution)/shard_map/pallas_call | solution.py:570
  51.5 0.2 collective-permute-start.7
  51.7 0.7 collective-permute-start.8
  52.3 0.5 collective-permute-done.7.r1a
  52.8 0.0 collective-permute-done.8.r1b
  52.8 1.0 %shard_map.103 = (f32[16,2,16,128]{3,2,1,0:T(8,128)S(1)}, f32[18,2,16,128]{3,2,1,0:T(8,128)S(1)}, f32[128,128]{1,0:T(8,128)S(1)}) custom-call(f32[20,8,128]{2,1,0:T(8,128)S(1)} %collective-permute-done.7.r1a, f32[16,2,8,128]{3,2,1,0:T(8,128)S(1)} %get-tuple-element.71.r1, f32[20,8,128]{2,1,0:T(8,128)S(1)} %collective-permute-done.8.r1b, ...), custom_call_target="tpu_custom_call" | custom-call | flops 6029312 | bytes 1507328 | tf_op jit(solution)/shard_map/pallas_call | solution.py:570
  53.8 13.0 %all_to_all.23 = f32[32,4,128]{2,1,0:T(4,128)S(1)} all-to-all(f32[32,4,128]{2,1,0:T(4,128)S(1)} %bitcast.11), channel_id=1, replica_groups=mesh['die'=4,'tile'=8] {'die','tile'}, dimensions={0} | all-to-all | bytes 131072 | tf_op jit(solution)/shard_map/all_to_all | solution.py:652
  66.8 0.0 copy-start
  66.8 3.8 %shard_map.104 = (f32[416,128]{1,0:T(8,128)S(1)}, f32[416,128]{1,0:T(8,128)S(1)}, f32[416,128]{1,0:T(8,128)S(1)}, f32[416,128]{1,0:T(8,128)S(1)}) custom-call(f32[128,128]{1,0:T(8,128)S(1)} %bitcast.9, f32[18,2,16,128]{3,2,1,0:T(8,128)S(1)} %get-tuple-element.73.w2, f32[16,2,16,128]{3,2,1,0:T(8,128)S(1)} %get-tuple-element.74.rx, ...), custom_call_target="tpu_custom_call" | custom-call | flops 30932992 | bytes 7733248 | tf_op jit(solution)/shard_map/pallas_call | solution.py:570
  70.6 0.8 collective-permute-start.10
  71.4 1.5 %collective-permute-start.11 = (f32[416,128]{1,0:T(8,128)S(1)}, f32[416,128]{1,0:T(8,128)S(1)}, u32[]{:S(2)}, u32[]{:S(2)}) collective-permute-start(f32[416,128]{1,0:T(8,128)S(1)} %get-tuple-element.79), channel_id=1, source_target_pairs={{0,24},{8,0},{16,8},{24,16},{1,25},{9,1},{17,9},{25,17},{2,26},{10... | collective-permute-start | bytes 638984 | tf_op jit(solution)/shard_map/ppermute | solution.py:585
  72.8 0.6 collective-permute-start.9
  73.4 0.6 shard_map.98
  74.0 3.9 %collective-permute-done.10.refs_2_ = f32[416,128]{1,0:T(8,128)S(1)} collective-permute-done((f32[416,128]{1,0:T(8,128)S(1)}, f32[416,128]{1,0:T(8,128)S(1)}, u32[]{:S(2)}, u32[]{:S(2)}) %collective-permute-start.10) | collective-permute-done | bytes 213024 | tf_op jit(solution)/shard_map/ppermute | solution.py:585
  78.0 1.5 %collective-permute-done.11.refs_3_ = f32[416,128]{1,0:T(8,128)S(1)} collective-permute-done((f32[416,128]{1,0:T(8,128)S(1)}, f32[416,128]{1,0:T(8,128)S(1)}, u32[]{:S(2)}, u32[]{:S(2)}) %collective-permute-start.11) | collective-permute-done | bytes 213024 | tf_op jit(solution)/shard_map/ppermute | solution.py:585
  79.5 4.2 %collective-permute-done.9.refs_1_ = f32[416,128]{1,0:T(8,128)S(1)} collective-permute-done((f32[416,128]{1,0:T(8,128)S(1)}, f32[416,128]{1,0:T(8,128)S(1)}, u32[]{:S(2)}, u32[]{:S(2)}) %collective-permute-start.9) | collective-permute-done | bytes 213024 | tf_op jit(solution)/shard_map/ppermute | solution.py:585
  83.7 0.0 copy-done
  83.7 1.3 %shard_map.105 = (f32[4,16,2048]{2,1,0:T(8,128)}, f32[4,16,2048]{2,1,0:T(8,128)}) custom-call(f32[4,16,2048]{2,1,0:T(8,128)S(1)} %copy-done, f32[16,8,128]{2,1,0:T(8,128)S(1)} %get-tuple-element.46.c, f32[16,8,128]{2,1,0:T(8,128)S(1)} %get-tuple-element.47.cu, f32[16,16,128]{2,1,0:T(8,128)S(1)} %get-tuple-element.48.up, ...), custom_call_target="tpu_custom_call" | custom-call | flops 11272192 | bytes 2818048 | tf_op jit(solution)/shard_map/pallas_call | solution.py:570
Async XLA Ops:
  2.5 9.2 %collective-permute-start = (f32[328,128]{1,0:T(8,128)S(1)}, f32[328,128]{1,0:T(8,128)S(1)}, u32[]{:S(2)}, u32[]{:S(2)}) collective-permute-start(f32[328,128]{1,0:T(8,128)S(1)} %get-tuple-element.42), channel_id=1, source_target_pairs={{0,8},{8,16},{16,24},{24,0},{1,9},{9,17},{17,25},{25,1},{2,10},{10... | collective-permute-start | bytes 503816 | tf_op jit(solution)/shard_map/ppermute | solution.py:585
  5.5 8.8 %collective-permute-start.1 = (f32[328,128]{1,0:T(8,128)S(1)}, f32[328,128]{1,0:T(8,128)S(1)}, u32[]{:S(2)}, u32[]{:S(2)}) collective-permute-start(f32[328,128]{1,0:T(8,128)S(1)} %get-tuple-element.43), channel_id=1, source_target_pairs={{0,16},{8,24},{16,0},{24,8},{1,17},{9,25},{17,1},{25,9},{2,18},{10... | collective-permute-start | bytes 503816 | tf_op jit(solution)/shard_map/ppermute | solution.py:585
  7.0 7.6 %collective-permute-start.2 = (f32[328,128]{1,0:T(8,128)S(1)}, f32[328,128]{1,0:T(8,128)S(1)}, u32[]{:S(2)}, u32[]{:S(2)}) collective-permute-start(f32[328,128]{1,0:T(8,128)S(1)} %get-tuple-element.44), channel_id=1, source_target_pairs={{0,24},{8,0},{16,8},{24,16},{1,25},{9,1},{17,9},{25,17},{2,26},{10... | collective-permute-start | bytes 503816 | tf_op jit(solution)/shard_map/ppermute | solution.py:585
  14.7 1.7 %collective-permute-start.3 = (f32[80,8,128]{2,1,0:T(8,128)S(1)}, f32[80,8,128]{2,1,0:T(8,128)S(1)}, u32[]{:S(2)}, u32[]{:S(2)}) collective-permute-start(f32[80,8,128]{2,1,0:T(8,128)S(1)} %get-tuple-element.50.one), channel_id=1, source_target_pairs={{0,1},{1,0},{2,3},{3,2},{4,5},{5,4},{6,7},{7,6},{8,9},{9,8},{10,11... | collective-permute-start | bytes 983048 | tf_op jit(solution)/shard_map/ppermute | solution.py:591
  14.8 1.6 %collective-permute-start.4 = (f32[80,8,128]{2,1,0:T(8,128)S(1)}, f32[80,8,128]{2,1,0:T(8,128)S(1)}, u32[]{:S(2)}, u32[]{:S(2)}) collective-permute-start(f32[80,8,128]{2,1,0:T(8,128)S(1)} %get-tuple-element.51.two), channel_id=1, source_target_pairs={{0,0},{1,2},{2,1},{3,4},{4,3},{5,6},{6,5},{7,7},{8,8},{9,10},{10,9... | collective-permute-start | bytes 983048 | tf_op jit(solution)/shard_map/ppermute | solution.py:591
  16.4 11.0 %copy-start.3 = (bf16[128,128]{1,0:T(8,128)(2,1)S(1)}, bf16[128,128]{1,0:T(8,128)(2,1)}, u32[]{:S(2)}) copy-start(bf16[128,128]{1,0:T(8,128)(2,1)} %constant.8.clone.down2) | copy-start | bytes 98308
  16.4 28.4 %copy-start.1 = (bf16[256,640]{1,0:T(8,128)(2,1)S(1)}, bf16[256,640]{1,0:T(8,128)(2,1)}, u32[]{:S(2)}) copy-start(bf16[256,640]{1,0:T(8,128)(2,1)} %constant.6.clone.spread1) | copy-start | bytes 983044
  16.4 28.3 %copy-start.2 = (bf16[128,256]{1,0:T(8,128)(2,1)S(1)}, bf16[128,256]{1,0:T(8,128)(2,1)}, u32[]{:S(2)}) copy-start(bf16[128,256]{1,0:T(8,128)(2,1)} %constant.7.clone.spread2) | copy-start | bytes 196612
  18.9 8.5 %collective-permute-start.5 = (f32[20,8,128]{2,1,0:T(8,128)S(1)}, f32[20,8,128]{2,1,0:T(8,128)S(1)}, u32[]{:S(2)}, u32[]{:S(2)}) collective-permute-start(f32[20,8,128]{2,1,0:T(8,128)S(1)} %get-tuple-element.57), channel_id=1, source_target_pairs={{0,1},{1,0},{2,3},{3,2},{4,5},{5,4},{6,7},{7,6},{8,9},{9,8},{10,11... | collective-permute-start | bytes 245768 | tf_op jit(solution)/shard_map/ppermute | solution.py:591
  26.2 1.2 %collective-permute-start.6 = (f32[20,8,128]{2,1,0:T(8,128)S(1)}, f32[20,8,128]{2,1,0:T(8,128)S(1)}, u32[]{:S(2)}, u32[]{:S(2)}) collective-permute-start(f32[20,8,128]{2,1,0:T(8,128)S(1)} %get-tuple-element.57), channel_id=1, source_target_pairs={{0,0},{1,2},{2,1},{3,4},{4,3},{5,6},{6,5},{7,7},{8,8},{9,10},{10,9... | collective-permute-start | bytes 245768 | tf_op jit(solution)/shard_map/ppermute | solution.py:591
  51.5 1.3 %collective-permute-start.7 = (f32[20,8,128]{2,1,0:T(8,128)S(1)}, f32[20,8,128]{2,1,0:T(8,128)S(1)}, u32[]{:S(2)}, u32[]{:S(2)}) collective-permute-start(f32[20,8,128]{2,1,0:T(8,128)S(1)} %get-tuple-element.70), channel_id=1, source_target_pairs={{0,1},{1,0},{2,3},{3,2},{4,5},{5,4},{6,7},{7,6},{8,9},{9,8},{10,11... | collective-permute-start | bytes 245768 | tf_op jit(solution)/shard_map/ppermute | solution.py:591
  51.7 1.2 %collective-permute-start.8 = (f32[20,8,128]{2,1,0:T(8,128)S(1)}, f32[20,8,128]{2,1,0:T(8,128)S(1)}, u32[]{:S(2)}, u32[]{:S(2)}) collective-permute-start(f32[20,8,128]{2,1,0:T(8,128)S(1)} %get-tuple-element.70), channel_id=1, source_target_pairs={{0,0},{1,2},{2,1},{3,4},{4,3},{5,6},{6,5},{7,7},{8,8},{9,10},{10,9... | collective-permute-start | bytes 245768 | tf_op jit(solution)/shard_map/ppermute | solution.py:591
  66.8 16.9 %copy-start = (f32[4,16,2048]{2,1,0:T(8,128)S(1)}, f32[4,16,2048]{2,1,0:T(8,128)}, u32[]{:S(2)}) copy-start(f32[4,16,2048]{2,1,0:T(8,128)} %f.1) | copy-start | bytes 1572868
  70.6 7.3 %collective-permute-start.10 = (f32[416,128]{1,0:T(8,128)S(1)}, f32[416,128]{1,0:T(8,128)S(1)}, u32[]{:S(2)}, u32[]{:S(2)}) collective-permute-start(f32[416,128]{1,0:T(8,128)S(1)} %get-tuple-element.78), channel_id=1, source_target_pairs={{0,16},{8,24},{16,0},{24,8},{1,17},{9,25},{17,1},{25,9},{2,18},{10... | collective-permute-start | bytes 638984 | tf_op jit(solution)/shard_map/ppermute | solution.py:585
  71.4 8.1 %collective-permute-start.11 = (f32[416,128]{1,0:T(8,128)S(1)}, f32[416,128]{1,0:T(8,128)S(1)}, u32[]{:S(2)}, u32[]{:S(2)}) collective-permute-start(f32[416,128]{1,0:T(8,128)S(1)} %get-tuple-element.79), channel_id=1, source_target_pairs={{0,24},{8,0},{16,8},{24,16},{1,25},{9,1},{17,9},{25,17},{2,26},{10... | collective-permute-start | bytes 638984 | tf_op jit(solution)/shard_map/ppermute | solution.py:585
  72.8 10.9 %collective-permute-start.9 = (f32[416,128]{1,0:T(8,128)S(1)}, f32[416,128]{1,0:T(8,128)S(1)}, u32[]{:S(2)}, u32[]{:S(2)}) collective-permute-start(f32[416,128]{1,0:T(8,128)S(1)} %get-tuple-element.77), channel_id=1, source_target_pairs={{0,8},{8,16},{16,24},{24,0},{1,9},{9,17},{17,25},{25,1},{2,10},{10... | collective-permute-start | bytes 638984 | tf_op jit(solution)/shard_map/ppermute | solution.py:585

commit v3 on v2

--- a/solution.py
+++ b/solution.py
@@ -297,7 +297,7 @@
             sums[z, :, tiles(j)] = (part[0] + part[1]) + (part[2] + part[3])
         return carry
 
-    lax.fori_loop(0, s.nz, body, 0)
+    lax.fori_loop(0, s.nz, body, 0, unroll=4)
     out = split_dot(sums[...].reshape(s.nz * s.r1, s.we), down[...])
     part = iota((s.r1, LN), 1) // (HX // 2)
     for g in range(s.nd):
@@ -333,7 +333,7 @@
                 va[z + 1, j, rows, :] = e0[z, j, rows, :] * x
         return carry
 
-    lax.fori_loop(0, s.nz, body, 0)
+    lax.fori_loop(0, s.nz, body, 0, unroll=4)
     level.sweep(va, v2, f, 1, s.re - 1)
     restrict(s, level, v2, f, HY - 4, s.re - HY + 4, down, rbuf, sums, r1, ship)
 
@@ -362,7 +362,7 @@
                 wa[z + 1, j, half:, :] = e1[z, j, half:, :] * down
         return carry
 
-    lax.fori_loop(0, s.nd, body, 0)
+    lax.fori_loop(0, s.nd, body, 0, unroll=2)
     level.sweep(wa, w2, rx, pad - 4, pad + own + 4)
 
     def put(z, j, rows, x):
@@ -410,7 +410,7 @@
             new.append((1.0 - OMEGA) * w + e2[z] * g)
         return tuple(new)
 
-    v = lax.fori_loop(0, NC - 1, body, tuple(v))
+    v = lax.fori_loop(0, NC - 1, body, tuple(v), unroll=True)
     for z in range(s.nz):
         cs[z, :HY, :] = jnp.zeros((HY, LN), F32)
         cs[z, HY + s.nt :, :] = jnp.zeros((HY, LN), F32)
@@ -434,7 +434,7 @@
                 wa[z + 1, j, rows, :] = jnp.where(level.scale[z, j, rows, :] > 0.0, y, 0.0)
         return carry
 
-    lax.fori_loop(0, s.nz, body, 0)
+    lax.fori_loop(0, s.nz, body, 0, unroll=4)
     level.sweep(wa, wb, rx, s.pad1 - 3, s.pad1 + s.own1 + 3)
     level.sweep(wb, wa, rx, s.pad1 - 2, s.pad1 + s.own1 + 2)
 
@@ -453,7 +453,7 @@
                 dst[z + 1, j, rows, :] = v[z + 1, j, rows, :] + jnp.where(upper, x[0], x[1])
         return carry
 
-    lax.fori_loop(0, s.nz, body, 0)
+    lax.fori_loop(0, s.nz, body, 0, unroll=4)
 
 
 def back_kernel(

time: 85.3 us -> 84.3 us (0.988)
  Pallas kernels: 19.6 us -> 18.6 us
    pallas_call x11, Pallas kernels: 19.5 us -> 18.5 us  [run(): pl.pallas_call(functools.partial(kernel, s), out_shape=shapes, in_specs=[...]
where the time goes in v3:
time: 84.3 us; the launch traced here: 84.1 us
  blocking collectives  29.4 us (35%)
  Pallas kernels  18.6 us (22%)
  starting transfers between devices  18.3 us (22%)
  waiting for transfers between devices  16.4 us (19%)
  between operations  1.42 us (2%)
    all_to_all x2, blocking collectives, everywhere(): return lax.all_to_all(send, ('die', 'tile'), 0, 0, tiled=True)  29.4 us
    pallas_call x11, Pallas kernels, run(): pl.pallas_call(functools.partial(kernel, s), out_shape=shapes, in_specs=[...  18.5 us
    ppermute x6, waiting for transfers between devices, shift(): return lax.ppermute(x, axis, [(i, (i + by) % n) for i in range(n)])  15.8 us
    ppermute x6, starting transfers between devices, swap(): lax.ppermute(x, 'tile', [(k, q if 0 <= q < n else k) for k, q in enumerat...  9.54 us
    ppermute x6, starting transfers between devices, shift(): return lax.ppermute(x, axis, [(i, (i + by) % n) for i in range(n)])  8.76 us
  transfers between devices with their start and end apart: 12, of which 7 were waited for; matrix products, arithmetic and copies ran while one was open for 0% of the time, Pallas kernels for 2%

profile of v3, /device:TPU:0, one launch (start us, length us, event | category | flops | bytes accessed | tf_op | source)
XLA Modules:
  0.0 84.1 jit_solution(5618243490678030046)
XLA Ops:
  1.3 1.2 %shard_map.95 = (f32[328,128]{1,0:T(8,128)S(1)}, f32[328,128]{1,0:T(8,128)S(1)}, f32[328,128]{1,0:T(8,128)S(1)}, f32[328,128]{1,0:T(8,128)S(1)}) custom-call(f32[6]{0:T(128)} %mat_h.1, s32[4]{0:T(128)} %material_h.1, f32[1,1]{1,0:T(1,128)} %bitcast.8.conductance_h, s32[4,24]{1,0:T(4,128)} %bitcast.13, f32[4,16,2048]{2,1,0:T(8,128)} %f.1), custom_call_target="tpu_custom_call" | custom-call | flops 4785840 | bytes 1196460 | tf_op jit(solution)/shard_map/pallas_call | solution.py:570
  2.5 3.0 %collective-permute-start = (f32[328,128]{1,0:T(8,128)S(1)}, f32[328,128]{1,0:T(8,128)S(1)}, u32[]{:S(2)}, u32[]{:S(2)}) collective-permute-start(f32[328,128]{1,0:T(8,128)S(1)} %get-tuple-element.42), channel_id=1, source_target_pairs={{0,8},{8,16},{16,24},{24,0},{1,9},{9,17},{17,25},{25,1},{2,10},{10... | collective-permute-start | bytes 503816 | tf_op jit(solution)/shard_map/ppermute | solution.py:585
  5.5 1.5 %collective-permute-start.1 = (f32[328,128]{1,0:T(8,128)S(1)}, f32[328,128]{1,0:T(8,128)S(1)}, u32[]{:S(2)}, u32[]{:S(2)}) collective-permute-start(f32[328,128]{1,0:T(8,128)S(1)} %get-tuple-element.43), channel_id=1, source_target_pairs={{0,16},{8,24},{16,0},{24,8},{1,17},{9,25},{17,1},{25,9},{2,18},{10... | collective-permute-start | bytes 503816 | tf_op jit(solution)/shard_map/ppermute | solution.py:585
  7.0 1.4 %collective-permute-start.2 = (f32[328,128]{1,0:T(8,128)S(1)}, f32[328,128]{1,0:T(8,128)S(1)}, u32[]{:S(2)}, u32[]{:S(2)}) collective-permute-start(f32[328,128]{1,0:T(8,128)S(1)} %get-tuple-element.44), channel_id=1, source_target_pairs={{0,24},{8,0},{16,8},{24,16},{1,25},{9,1},{17,9},{25,17},{2,26},{10... | collective-permute-start | bytes 503816 | tf_op jit(solution)/shard_map/ppermute | solution.py:585
  8.5 3.2 %collective-permute-done.refs_1_ = f32[328,128]{1,0:T(8,128)S(1)} collective-permute-done((f32[328,128]{1,0:T(8,128)S(1)}, f32[328,128]{1,0:T(8,128)S(1)}, u32[]{:S(2)}, u32[]{:S(2)}) %collective-permute-start) | collective-permute-done | bytes 167968 | tf_op jit(solution)/shard_map/ppermute | solution.py:585
  11.6 2.7 %collective-permute-done.1.refs_2_ = f32[328,128]{1,0:T(8,128)S(1)} collective-permute-done((f32[328,128]{1,0:T(8,128)S(1)}, f32[328,128]{1,0:T(8,128)S(1)}, u32[]{:S(2)}, u32[]{:S(2)}) %collective-permute-start.1) | collective-permute-done | bytes 167968 | tf_op jit(solution)/shard_map/ppermute | solution.py:585
  14.3 0.3 collective-permute-done.2.refs_3_
  14.6 0.1 shard_map.96
  14.7 0.1 collective-permute-start.3
  14.8 0.7 collective-permute-start.4
  15.5 0.1 down.1
  15.5 0.8 shard_map.97
  16.4 0.0 collective-permute-done.3.from_one
  16.4 0.0 collective-permute-done.4.from_two
  16.4 0.0 copy-start.3
  16.4 0.0 copy-start.1
  16.4 0.0 copy-start.2
  16.4 2.4 %shard_map.99 = (f32[16,5,32,128]{3,2,1,0:T(8,128)S(1)}, f32[18,5,32,128]{3,2,1,0:T(8,128)S(1)}, f32[16,2,8,128]{3,2,1,0:T(8,128)S(1)}, f32[20,8,128]{2,1,0:T(8,128)S(1)}) custom-call(f32[80,8,128]{2,1,0:T(8,128)S(1)} %collective-permute-done.3.from_one, f32[80,8,128]{2,1,0:T(8,128)S(1)} %collective-permute-done.4.from_two, ...), custom_call_target="tpu_custom_call" | custom-call | flops 28508160 | bytes 7127040 | tf_op jit(solution)/shard_map/pallas_call | solution.py:570
  18.8 7.3 %collective-permute-start.5 = (f32[20,8,128]{2,1,0:T(8,128)S(1)}, f32[20,8,128]{2,1,0:T(8,128)S(1)}, u32[]{:S(2)}, u32[]{:S(2)}) collective-permute-start(f32[20,8,128]{2,1,0:T(8,128)S(1)} %get-tuple-element.57), channel_id=1, source_target_pairs={{0,1},{1,0},{2,3},{3,2},{4,5},{5,4},{6,7},{7,6},{8,9},{9,8},{10,11... | collective-permute-start | bytes 245768 | tf_op jit(solution)/shard_map/ppermute | solution.py:591
  26.1 0.7 collective-permute-start.6
  26.7 0.5 shard_map.100
  27.3 0.0 collective-permute-done.5.r1a
  27.3 0.0 collective-permute-done.6.r1b
  27.3 0.0 copy-done.3
  27.3 0.8 %shard_map.101 = (f32[16,2,16,128]{3,2,1,0:T(8,128)S(1)}, f32[18,2,16,128]{3,2,1,0:T(8,128)S(1)}, f32[128,128]{1,0:T(8,128)S(1)}) custom-call(f32[20,8,128]{2,1,0:T(8,128)S(1)} %collective-permute-done.5.r1a, f32[16,2,8,128]{3,2,1,0:T(8,128)S(1)} %get-tuple-element.58.r1, f32[20,8,128]{2,1,0:T(8,128)S(1)} %collective-permute-done.6.r1b, ...), custom_call_target="tpu_custom_call" | custom-call | flops 6029312 | bytes 1507328 | tf_op jit(solution)/shard_map/pallas_call | solution.py:570
  28.1 16.4 %all_to_all.22 = f32[32,4,128]{2,1,0:T(4,128)S(1)} all-to-all(f32[32,4,128]{2,1,0:T(4,128)S(1)} %bitcast.12), channel_id=1, replica_groups=mesh['die'=4,'tile'=8] {'die','tile'}, dimensions={0} | all-to-all | bytes 131072 | tf_op jit(solution)/shard_map/all_to_all | solution.py:652
  44.5 0.0 copy-done.1
  44.5 0.0 copy-done.2
  44.5 6.4 %shard_map.102 = (f32[18,5,32,128]{3,2,1,0:T(8,128)S(1)}, f32[16,2,8,128]{3,2,1,0:T(8,128)S(1)}, f32[20,8,128]{2,1,0:T(8,128)S(1)}) custom-call(f32[128,128]{1,0:T(8,128)S(1)} %bitcast.10, f32[18,5,32,128]{3,2,1,0:T(8,128)S(1)} %get-tuple-element.63.v2, f32[16,5,32,128]{3,2,1,0:T(8,128)S(1)} %get-tuple-element.64.f, ...), custom_call_target="tpu_custom_call" | custom-call | flops 36896768 | bytes 9224192 | tf_op jit(solution)/shard_map/pallas_call | solution.py:570
  50.9 0.2 collective-permute-start.7
  51.1 0.7 collective-permute-start.8
  51.7 0.5 collective-permute-done.7.r1a
  52.2 0.0 collective-permute-done.8.r1b
  52.2 0.8 shard_map.103
  53.1 13.0 %all_to_all.23 = f32[32,4,128]{2,1,0:T(4,128)S(1)} all-to-all(f32[32,4,128]{2,1,0:T(4,128)S(1)} %bitcast.11), channel_id=1, replica_groups=mesh['die'=4,'tile'=8] {'die','tile'}, dimensions={0} | all-to-all | bytes 131072 | tf_op jit(solution)/shard_map/all_to_all | solution.py:652
  66.1 0.0 copy-start
  66.1 3.6 %shard_map.104 = (f32[416,128]{1,0:T(8,128)S(1)}, f32[416,128]{1,0:T(8,128)S(1)}, f32[416,128]{1,0:T(8,128)S(1)}, f32[416,128]{1,0:T(8,128)S(1)}) custom-call(f32[128,128]{1,0:T(8,128)S(1)} %bitcast.9, f32[18,2,16,128]{3,2,1,0:T(8,128)S(1)} %get-tuple-element.73.w2, f32[16,2,16,128]{3,2,1,0:T(8,128)S(1)} %get-tuple-element.74.rx, ...), custom_call_target="tpu_custom_call" | custom-call | flops 30932992 | bytes 7733248 | tf_op jit(solution)/shard_map/pallas_call | solution.py:570
  69.7 0.8 collective-permute-start.10
  70.4 1.4 %collective-permute-start.11 = (f32[416,128]{1,0:T(8,128)S(1)}, f32[416,128]{1,0:T(8,128)S(1)}, u32[]{:S(2)}, u32[]{:S(2)}) collective-permute-start(f32[416,128]{1,0:T(8,128)S(1)} %get-tuple-element.79), channel_id=1, source_target_pairs={{0,24},{8,0},{16,8},{24,16},{1,25},{9,1},{17,9},{25,17},{2,26},{10... | collective-permute-start | bytes 638984 | tf_op jit(solution)/shard_map/ppermute | solution.py:585
  71.9 0.6 collective-permute-start.9
  72.5 0.6 shard_map.98
  73.1 3.9 %collective-permute-done.10.refs_2_ = f32[416,128]{1,0:T(8,128)S(1)} collective-permute-done((f32[416,128]{1,0:T(8,128)S(1)}, f32[416,128]{1,0:T(8,128)S(1)}, u32[]{:S(2)}, u32[]{:S(2)}) %collective-permute-start.10) | collective-permute-done | bytes 213024 | tf_op jit(solution)/shard_map/ppermute | solution.py:585
  77.0 1.5 %collective-permute-done.11.refs_3_ = f32[416,128]{1,0:T(8,128)S(1)} collective-permute-done((f32[416,128]{1,0:T(8,128)S(1)}, f32[416,128]{1,0:T(8,128)S(1)}, u32[]{:S(2)}, u32[]{:S(2)}) %collective-permute-start.11) | collective-permute-done | bytes 213024 | tf_op jit(solution)/shard_map/ppermute | solution.py:585
  78.5 4.2 %collective-permute-done.9.refs_1_ = f32[416,128]{1,0:T(8,128)S(1)} collective-permute-done((f32[416,128]{1,0:T(8,128)S(1)}, f32[416,128]{1,0:T(8,128)S(1)}, u32[]{:S(2)}, u32[]{:S(2)}) %collective-permute-start.9) | collective-permute-done | bytes 213024 | tf_op jit(solution)/shard_map/ppermute | solution.py:585
  82.7 0.0 copy-done
  82.8 1.3 %shard_map.105 = (f32[4,16,2048]{2,1,0:T(8,128)}, f32[4,16,2048]{2,1,0:T(8,128)}) custom-call(f32[4,16,2048]{2,1,0:T(8,128)S(1)} %copy-done, f32[16,8,128]{2,1,0:T(8,128)S(1)} %get-tuple-element.46.c, f32[16,8,128]{2,1,0:T(8,128)S(1)} %get-tuple-element.47.cu, f32[16,16,128]{2,1,0:T(8,128)S(1)} %get-tuple-element.48.up, ...), custom_call_target="tpu_custom_call" | custom-call | flops 11272192 | bytes 2818048 | tf_op jit(solution)/shard_map/pallas_call | solution.py:570
Async XLA Ops:
  2.5 9.2 %collective-permute-start = (f32[328,128]{1,0:T(8,128)S(1)}, f32[328,128]{1,0:T(8,128)S(1)}, u32[]{:S(2)}, u32[]{:S(2)}) collective-permute-start(f32[328,128]{1,0:T(8,128)S(1)} %get-tuple-element.42), channel_id=1, source_target_pairs={{0,8},{8,16},{16,24},{24,0},{1,9},{9,17},{17,25},{25,1},{2,10},{10... | collective-permute-start | bytes 503816 | tf_op jit(solution)/shard_map/ppermute | solution.py:585
  5.5 8.8 %collective-permute-start.1 = (f32[328,128]{1,0:T(8,128)S(1)}, f32[328,128]{1,0:T(8,128)S(1)}, u32[]{:S(2)}, u32[]{:S(2)}) collective-permute-start(f32[328,128]{1,0:T(8,128)S(1)} %get-tuple-element.43), channel_id=1, source_target_pairs={{0,16},{8,24},{16,0},{24,8},{1,17},{9,25},{17,1},{25,9},{2,18},{10... | collective-permute-start | bytes 503816 | tf_op jit(solution)/shard_map/ppermute | solution.py:585
  7.0 7.6 %collective-permute-start.2 = (f32[328,128]{1,0:T(8,128)S(1)}, f32[328,128]{1,0:T(8,128)S(1)}, u32[]{:S(2)}, u32[]{:S(2)}) collective-permute-start(f32[328,128]{1,0:T(8,128)S(1)} %get-tuple-element.44), channel_id=1, source_target_pairs={{0,24},{8,0},{16,8},{24,16},{1,25},{9,1},{17,9},{25,17},{2,26},{10... | collective-permute-start | bytes 503816 | tf_op jit(solution)/shard_map/ppermute | solution.py:585
  14.7 1.7 %collective-permute-start.3 = (f32[80,8,128]{2,1,0:T(8,128)S(1)}, f32[80,8,128]{2,1,0:T(8,128)S(1)}, u32[]{:S(2)}, u32[]{:S(2)}) collective-permute-start(f32[80,8,128]{2,1,0:T(8,128)S(1)} %get-tuple-element.50.one), channel_id=1, source_target_pairs={{0,1},{1,0},{2,3},{3,2},{4,5},{5,4},{6,7},{7,6},{8,9},{9,8},{10,11... | collective-permute-start | bytes 983048 | tf_op jit(solution)/shard_map/ppermute | solution.py:591
  14.8 1.6 %collective-permute-start.4 = (f32[80,8,128]{2,1,0:T(8,128)S(1)}, f32[80,8,128]{2,1,0:T(8,128)S(1)}, u32[]{:S(2)}, u32[]{:S(2)}) collective-permute-start(f32[80,8,128]{2,1,0:T(8,128)S(1)} %get-tuple-element.51.two), channel_id=1, source_target_pairs={{0,0},{1,2},{2,1},{3,4},{4,3},{5,6},{6,5},{7,7},{8,8},{9,10},{10,9... | collective-permute-start | bytes 983048 | tf_op jit(solution)/shard_map/ppermute | solution.py:591
  16.4 10.9 %copy-start.3 = (bf16[128,128]{1,0:T(8,128)(2,1)S(1)}, bf16[128,128]{1,0:T(8,128)(2,1)}, u32[]{:S(2)}) copy-start(bf16[128,128]{1,0:T(8,128)(2,1)} %constant.8.clone.down2) | copy-start | bytes 98308
  16.4 28.1 %copy-start.1 = (bf16[256,640]{1,0:T(8,128)(2,1)S(1)}, bf16[256,640]{1,0:T(8,128)(2,1)}, u32[]{:S(2)}) copy-start(bf16[256,640]{1,0:T(8,128)(2,1)} %constant.6.clone.spread1) | copy-start | bytes 983044
  16.4 28.1 %copy-start.2 = (bf16[128,256]{1,0:T(8,128)(2,1)S(1)}, bf16[128,256]{1,0:T(8,128)(2,1)}, u32[]{:S(2)}) copy-start(bf16[128,256]{1,0:T(8,128)(2,1)} %constant.7.clone.spread2) | copy-start | bytes 196612
  18.8 8.5 %collective-permute-start.5 = (f32[20,8,128]{2,1,0:T(8,128)S(1)}, f32[20,8,128]{2,1,0:T(8,128)S(1)}, u32[]{:S(2)}, u32[]{:S(2)}) collective-permute-start(f32[20,8,128]{2,1,0:T(8,128)S(1)} %get-tuple-element.57), channel_id=1, source_target_pairs={{0,1},{1,0},{2,3},{3,2},{4,5},{5,4},{6,7},{7,6},{8,9},{9,8},{10,11... | collective-permute-start | bytes 245768 | tf_op jit(solution)/shard_map/ppermute | solution.py:591
  26.1 1.2 %collective-permute-start.6 = (f32[20,8,128]{2,1,0:T(8,128)S(1)}, f32[20,8,128]{2,1,0:T(8,128)S(1)}, u32[]{:S(2)}, u32[]{:S(2)}) collective-permute-start(f32[20,8,128]{2,1,0:T(8,128)S(1)} %get-tuple-element.57), channel_id=1, source_target_pairs={{0,0},{1,2},{2,1},{3,4},{4,3},{5,6},{6,5},{7,7},{8,8},{9,10},{10,9... | collective-permute-start | bytes 245768 | tf_op jit(solution)/shard_map/ppermute | solution.py:591
  50.9 1.3 %collective-permute-start.7 = (f32[20,8,128]{2,1,0:T(8,128)S(1)}, f32[20,8,128]{2,1,0:T(8,128)S(1)}, u32[]{:S(2)}, u32[]{:S(2)}) collective-permute-start(f32[20,8,128]{2,1,0:T(8,128)S(1)} %get-tuple-element.70), channel_id=1, source_target_pairs={{0,1},{1,0},{2,3},{3,2},{4,5},{5,4},{6,7},{7,6},{8,9},{9,8},{10,11... | collective-permute-start | bytes 245768 | tf_op jit(solution)/shard_map/ppermute | solution.py:591
  51.1 1.2 %collective-permute-start.8 = (f32[20,8,128]{2,1,0:T(8,128)S(1)}, f32[20,8,128]{2,1,0:T(8,128)S(1)}, u32[]{:S(2)}, u32[]{:S(2)}) collective-permute-start(f32[20,8,128]{2,1,0:T(8,128)S(1)} %get-tuple-element.70), channel_id=1, source_target_pairs={{0,0},{1,2},{2,1},{3,4},{4,3},{5,6},{6,5},{7,7},{8,8},{9,10},{10,9... | collective-permute-start | bytes 245768 | tf_op jit(solution)/shard_map/ppermute | solution.py:591
  66.1 16.7 %copy-start = (f32[4,16,2048]{2,1,0:T(8,128)S(1)}, f32[4,16,2048]{2,1,0:T(8,128)}, u32[]{:S(2)}) copy-start(f32[4,16,2048]{2,1,0:T(8,128)} %f.1) | copy-start | bytes 1572868
  69.7 7.3 %collective-permute-start.10 = (f32[416,128]{1,0:T(8,128)S(1)}, f32[416,128]{1,0:T(8,128)S(1)}, u32[]{:S(2)}, u32[]{:S(2)}) collective-permute-start(f32[416,128]{1,0:T(8,128)S(1)} %get-tuple-element.78), channel_id=1, source_target_pairs={{0,16},{8,24},{16,0},{24,8},{1,17},{9,25},{17,1},{25,9},{2,18},{10... | collective-permute-start | bytes 638984 | tf_op jit(solution)/shard_map/ppermute | solution.py:585
  70.4 8.1 %collective-permute-start.11 = (f32[416,128]{1,0:T(8,128)S(1)}, f32[416,128]{1,0:T(8,128)S(1)}, u32[]{:S(2)}, u32[]{:S(2)}) collective-permute-start(f32[416,128]{1,0:T(8,128)S(1)} %get-tuple-element.79), channel_id=1, source_target_pairs={{0,24},{8,0},{16,8},{24,16},{1,25},{9,1},{17,9},{25,17},{2,26},{10... | collective-permute-start | bytes 638984 | tf_op jit(solution)/shard_map/ppermute | solution.py:585
  71.9 10.9 %collective-permute-start.9 = (f32[416,128]{1,0:T(8,128)S(1)}, f32[416,128]{1,0:T(8,128)S(1)}, u32[]{:S(2)}, u32[]{:S(2)}) collective-permute-start(f32[416,128]{1,0:T(8,128)S(1)} %get-tuple-element.77), channel_id=1, source_target_pairs={{0,8},{8,16},{16,24},{24,0},{1,9},{9,17},{17,25},{25,1},{2,10},{10... | collective-permute-start | bytes 638984 | tf_op jit(solution)/shard_map/ppermute | solution.py:585
